TPU v7x, 32 devices: a whole 2x2x4 slice. The times are simulated.
32 devices in a mesh: dp: 4 (over z), seq: 4 (over y, x), head: 2 (over core).
Axes of the slice: x: 2, y: 2, z: 4, core: 2. Of those that a mesh axis runs over, the one named last changes fastest.
Arguments:
- block_input: float32 [8, 1024, 1024], P('dp', 'seq', 'head'), may hold values from -6 to 6
- segment_ids: int32 [8, 1024], P('dp', 'seq'), may hold values from 0 to 3, never falling along the last dimension, each value on 1 to 512 neighbouring positions
- mixer_gain: float32 [1024], replicated, may hold values from 0.5 to 1.5
- query_weight: bfloat16 [1024, 1024], P(None, 'head'), may hold values from -0.1875 to 0.1875
- key_weight: bfloat16 [1024, 1024], P(None, 'head'), may hold values from -0.1875 to 0.1875
- value_weight: bfloat16 [1024, 1024], P(None, 'head'), may hold values from -0.1875 to 0.1875
- gate_weight: bfloat16 [1024, 1024], P(None, 'head'), may hold values from -0.1875 to 0.1875
- beta_weight: bfloat16 [1024, 8], P(None, 'head'), may hold values from -0.1875 to 0.1875
- conv_weight: float32 [3, 4, 8, 128], P(None, None, 'head'), may hold values from -3 to 3
- head_gain: float32 [128], replicated, may hold values from 0.5 to 1.5
- out_weight: bfloat16 [1024, 1024], P('head'), may hold values from -0.375 to 0.375
- feed_gain: float32 [1024], replicated, may hold values from 0.5 to 1.5
- feed_gate: bfloat16 [1024, 2816], P(None, 'head'), may hold values from -0.1875 to 0.1875
- feed_up: bfloat16 [1024, 2816], P(None, 'head'), may hold values from -0.1875 to 0.1875
- feed_down: bfloat16 [2816, 1024], P('head'), may hold values from -0.21875 to 0.21875
- grad_output: float32 [8, 1024, 1024], P('dp', 'seq', 'head'), may hold values from -6 to 6
Outputs:
- block_output: float32 [8, 1024, 1024], P('dp', 'seq', 'head')
- input_grad: float32 [8, 1024, 1024], P('dp', 'seq', 'head')
- grad_mixer_gain: float32 [1024], P(('dp', 'seq'))
- grad_query: float32 [1024, 1024], P(('dp', 'seq'), 'head')
- grad_key: float32 [1024, 1024], P(('dp', 'seq'), 'head')
- grad_value: float32 [1024, 1024], P(('dp', 'seq'), 'head')
- grad_gate: float32 [1024, 1024], P(('dp', 'seq'), 'head')
- grad_beta: float32 [1024, 8], P(('dp', 'seq'), 'head')
- grad_conv: float32 [3, 4, 8, 128], P(None, None, 'head', ('dp', 'seq'))
- grad_head_gain: float32 [128], P(('dp', 'seq'))
- grad_out_weight: float32 [1024, 1024], P('head', ('dp', 'seq'))
- grad_feed_gain: float32 [1024], P(('dp', 'seq'))
- grad_feed_gate: float32 [1024, 2816], P(('dp', 'seq'), 'head')
- grad_feed_up: float32 [1024, 2816], P(('dp', 'seq'), 'head')
- grad_feed_down: float32 [2816, 1024], P('head', ('dp', 'seq'))
Inputs may be any that keep to these rules, and one draw needn't show every extreme that they name: `segment_ids`: in each sequence the ids never fall; a document is a run of equal ids, and the first token of a sequence starts one.
All inputs are finite; a program needn't handle non-finite values.
Results may differ from a plain program's by a relative error of at most 0.012.
Values sent between devices are 32-bit elements; how exact they have to be, the bound alone decides.
No kernel may reach another device: no remote copies, remote signals or barrier semaphores. Data moves between devices by JAX's collectives and lax.ppermute only.
A program may use at most 192 MiB of HBM per device.

v0:
```python
import math

import jax
import jax.numpy as jnp
from jax import lax
from jax.sharding import PartitionSpec as P

GROUP = 64


norm_eps = 1e-05
unit_eps = 1e-06
top_precision = lax.Precision.HIGHEST


def from_behind(value, axis, steps):
    count = lax.axis_size(axis)
    initial, last = (max(0, -steps), min(count, count - steps))
    return lax.ppermute(value, axis, [(source, source + steps) for source in range(initial, last)])


def entering(value, axis, combine, identity, reverse):
    length, position = (lax.axis_size(axis), lax.axis_index(axis))
    everything = jax.tree.map(lambda part: lax.all_gather(part, axis), value)
    start = jax.tree.map(
        lambda part, zero: jnp.broadcast_to(jnp.asarray(zero, part.dtype), part.shape),
        value,
        identity,
    )

    def turn(k, before):
        at = length - 1 - k if reverse else k
        reached = at > position if reverse else at < position
        new = combine(before, jax.tree.map(lambda part: part[at], everything))
        return jax.tree.map(lambda a, b: jnp.where(reached, a, b), new, before)

    return lax.fori_loop(0, length, turn, start)


def batch_mul(first_op, second_op):
    return jnp.einsum("...ij,...jk->...ik", first_op, second_op, precision=top_precision)


def compose(earlier_pair, later_pair):
    return (
        batch_mul(earlier_pair[0], later_pair[0]),
        batch_mul(earlier_pair[1], later_pair[0]) + later_pair[1],
    )


def rms_scale(values):
    return lax.rsqrt(jnp.mean(values * values, axis=-1, keepdims=True) + norm_eps)


def unit_rows(values):
    return values * lax.rsqrt(jnp.sum(values * values, axis=-1, keepdims=True) + unit_eps)


def bf_round(values):
    return lax.optimization_barrier(values.astype(jnp.bfloat16)).astype(jnp.float32)


def silu_slope(values):
    sigmoid_value = jax.nn.sigmoid(values)
    return sigmoid_value * (1.0 + values * (1.0 - sigmoid_value))


def norm_back(grad_rows, normed, row_scale, gain_vec):
    grad_hat = grad_rows * gain_vec
    return row_scale * (grad_hat - normed * jnp.mean(grad_hat * normed, axis=-1, keepdims=True))


def matmul(first_op, second_op):
    return jnp.dot(first_op, second_op, preferred_element_type=jnp.float32)


def matmul_back(first_op, second_op):
    return lax.dot_general(
        first_op, second_op, (((0,), (0,)), ((), ())), preferred_element_type=jnp.float32
    )


def matmul_right_t(first_op, second_op):
    return lax.dot_general(
        first_op, second_op, (((1,), (1,)), ((), ())), preferred_element_type=jnp.float32
    )


def to_blocks(values, block_size):
    seq_count, tok_count, head_count, feature_width = values.shape
    shaped = values.reshape(
        seq_count, tok_count // block_size, block_size, head_count, feature_width
    )
    return shaped.transpose(1, 0, 3, 2, 4)


def from_blocks(values):
    block_count, seq_count, head_count, block_size, feature_width = values.shape
    return values.transpose(1, 0, 3, 2, 4).reshape(
        seq_count * block_count * block_size, head_count * feature_width
    )


def local(
    block_input,
    segment_ids,
    mixer_gain,
    query_weight,
    key_weight,
    value_weight,
    gate_weight,
    beta_weight,
    conv_weight,
    head_gain,
    out_weight,
    feed_gain,
    feed_gate,
    feed_up,
    feed_down,
    grad_output,
):
    seq_count, tok_count, half_width = block_input.shape
    row_count = seq_count * tok_count
    key_size = head_gain.shape[0]
    head_local = beta_weight.shape[1]
    channels = query_weight.shape[1]
    model_width = query_weight.shape[0]
    block_count = tok_count // GROUP
    tap_count = conv_weight.shape[1]
    delay_rows = tap_count - 1
    query_factor = 1.0 / math.sqrt(key_size)
    full_input = lax.all_gather(block_input, "head", axis=2, tiled=True).reshape(
        row_count, model_width
    )
    input_scale = rms_scale(full_input)
    input_normed = full_input * input_scale
    normed_in = (input_normed * mixer_gain).astype(jnp.bfloat16)
    query_proj = matmul(normed_in, query_weight)
    key_proj = matmul(normed_in, key_weight)
    value_proj = matmul(normed_in, value_weight)
    gate_proj = matmul(normed_in, gate_weight)
    beta_logits = matmul(normed_in, beta_weight)
    stacked = jnp.stack([query_proj, key_proj, value_proj]).reshape(
        3, seq_count, tok_count, channels
    )
    segment_float = segment_ids.astype(jnp.float32)
    edge_rows, edge_ids = from_behind(
        (stacked[:, :, tok_count - delay_rows :, :], segment_float[:, tok_count - delay_rows :]),
        "seq",
        1,
    )
    extended_ids = jnp.concatenate([edge_ids, segment_float], axis=1)
    tap_masks = [
        (extended_ids[:, tap_index : tap_index + tok_count] == segment_float).astype(jnp.float32)[
            None, :, :, None
        ]
        for tap_index in range(tap_count)
    ]
    conv_taps = conv_weight.reshape(3, tap_count, channels)

    def conv_heads(stacked_in, edge_in, taps_in):
        extended = jnp.concatenate([edge_in, stacked_in], axis=2)
        mixed_sum = taps_in[:, 0, None, None, :] * extended[:, :, 0:tok_count, :] * tap_masks[0]
        for tap_index in range(1, tap_count):
            mixed_sum = (
                mixed_sum
                + taps_in[:, tap_index, None, None, :]
                * extended[:, :, tap_index : tap_index + tok_count, :]
                * tap_masks[tap_index]
            )
        active = jax.nn.silu(mixed_sum).reshape(3, seq_count, tok_count, head_local, key_size)
        query_heads = unit_rows(active[0]) * query_factor
        key_heads = unit_rows(active[1])
        return (
            to_blocks(query_heads, GROUP),
            to_blocks(key_heads, GROUP),
            to_blocks(active[2], GROUP),
        )

    (query_raw, key_raw, value_raw), conv_back = jax.vjp(conv_heads, stacked, edge_rows, conv_taps)
    query_blk = bf_round(query_raw)
    key_blk = bf_round(key_raw)
    value_blk = bf_round(value_raw)

    def beta_blocks(logits):
        gate_values = jax.nn.sigmoid(logits).reshape(seq_count, block_count, GROUP, head_local)
        return gate_values.transpose(1, 0, 3, 2)

    beta_blk, beta_back = jax.vjp(beta_blocks, beta_logits)
    segment_blk = segment_float.reshape(seq_count, block_count, GROUP).transpose(1, 0, 2)
    prior_ids = jnp.concatenate(
        [edge_ids[None, :, delay_rows - 1], segment_blk[:-1, :, GROUP - 1]], axis=0
    )
    same_blk = (segment_blk[:, :, :, None] == segment_blk[:, :, None, :]).astype(jnp.float32)[
        :, :, None
    ]
    enter_blk = (segment_blk == prior_ids[:, :, None]).astype(jnp.float32)[:, :, None]
    last_blk = (segment_blk == segment_blk[:, :, GROUP - 1 :]).astype(jnp.float32)[:, :, None]
    enter_last = enter_blk[..., GROUP - 1]
    eye_block = jnp.eye(GROUP, dtype=jnp.float32)
    causal = jnp.tril(jnp.ones((GROUP, GROUP), jnp.float32))
    eye_key = jnp.eye(key_size, dtype=jnp.float32)

    def block_prep(key_in, value_in, beta_in):
        key_inner = jnp.einsum("nshcd,nshjd->nshcj", key_in, key_in, precision=top_precision)
        system = eye_block + jnp.tril(beta_in[..., :, None] * key_inner * same_blk, -1)
        right_side = jnp.concatenate(
            [beta_in[..., None] * value_in, (beta_in * enter_blk)[..., None] * key_in], axis=-1
        )
        solved = jax.scipy.linalg.solve_triangular(
            system, right_side, lower=True, unit_diagonal=True
        )
        base_update = solved[..., :key_size]
        carry_weight = solved[..., key_size:]
        masked_keys = last_blk[..., None] * key_in
        transit = enter_last[..., None, None] * eye_key - jnp.einsum(
            "nshcj,nshck->nshjk", carry_weight, masked_keys, precision=top_precision
        )
        fresh_state = jnp.einsum(
            "nshcv,nshck->nshvk", base_update, masked_keys, precision=top_precision
        )
        return (base_update, carry_weight, transit, fresh_state)

    (base_update, carry_weight, transit, fresh_state), prep_back = jax.vjp(
        block_prep, key_blk, value_blk, beta_blk
    )
    eye_state = jnp.broadcast_to(eye_key, (seq_count, head_local, key_size, key_size))
    zero_state = jnp.zeros((seq_count, head_local, key_size, key_size), jnp.float32)

    def chain_step(carried, pieces):
        return (compose(carried, pieces), None)

    chained, unused = lax.scan(chain_step, (eye_state, zero_state), (transit, fresh_state))
    device_transit, device_fresh = chained
    prefix_pair = entering(
        (device_transit, device_fresh), "seq", compose, (eye_state, zero_state), False
    )
    state_in = prefix_pair[1]

    def read_out(query_in, key_in, base_in, weight_in, transit_in, fresh_in, start_state):

        def one_block(state_now, pieces):
            (
                query_one,
                key_one,
                base_one,
                weight_one,
                transit_one,
                fresh_one,
                same_one,
                enter_one,
            ) = pieces
            update = base_one - jnp.einsum(
                "shck,shvk->shcv", weight_one, state_now, precision=top_precision
            )
            attend = (
                jnp.einsum("shck,shjk->shcj", query_one, key_one, precision=top_precision)
                * same_one
                * causal
            )
            output = enter_one[..., None] * jnp.einsum(
                "shck,shvk->shcv", query_one, state_now, precision=top_precision
            ) + jnp.einsum("shcj,shjv->shcv", attend, update, precision=top_precision)
            return (batch_mul(state_now, transit_one) + fresh_one, output)

        final_state, outputs = lax.scan(
            one_block,
            start_state,
            (query_in, key_in, base_in, weight_in, transit_in, fresh_in, same_blk, enter_blk),
        )
        return (from_blocks(outputs), final_state)

    (mix_rows, state_out), read_back = jax.vjp(
        read_out, query_blk, key_blk, base_update, carry_weight, transit, fresh_state, state_in
    )

    def gate_norm(mix_in, gain_in, gate_in):
        shaped = mix_in.reshape(row_count, head_local, key_size)
        gate_values = jax.nn.silu(gate_in.reshape(row_count, head_local, key_size))
        return (shaped * rms_scale(shaped) * gain_in * gate_values).reshape(row_count, channels)

    gated_rows, gate_back = jax.vjp(gate_norm, mix_rows, head_gain, gate_proj)
    gated_low = gated_rows.astype(jnp.bfloat16)
    mixer_part = matmul(gated_low, out_weight).reshape(seq_count, tok_count, model_width)
    mixer_share = lax.psum_scatter(mixer_part, "head", scatter_dimension=2, tiled=True)
    middle_share = block_input + mixer_share
    middle_full = lax.all_gather(middle_share, "head", axis=2, tiled=True).reshape(
        row_count, model_width
    )
    middle_scale = rms_scale(middle_full)
    middle_normed = middle_full * middle_scale
    normed_mid = (middle_normed * feed_gain).astype(jnp.bfloat16)
    gate_act = matmul(normed_mid, feed_gate)
    up_act = matmul(normed_mid, feed_up)
    gate_silu = jax.nn.silu(gate_act)
    inner_low = (gate_silu * up_act).astype(jnp.bfloat16)
    down_part = matmul(inner_low, feed_down).reshape(seq_count, tok_count, model_width)
    block_output = middle_share + lax.psum_scatter(
        down_part, "head", scatter_dimension=2, tiled=True
    )
    grad_full = lax.all_gather(grad_output, "head", axis=2, tiled=True).reshape(
        row_count, model_width
    )
    down_grad = grad_full.astype(jnp.bfloat16)
    inner_grad = matmul_right_t(down_grad, feed_down)
    grad_feed_down = matmul_back(inner_low, down_grad)
    gate_grad = (inner_grad * up_act * silu_slope(gate_act)).astype(jnp.bfloat16)
    up_grad = (inner_grad * gate_silu).astype(jnp.bfloat16)
    grad_feed_gate = matmul_back(normed_mid, gate_grad)
    grad_feed_up = matmul_back(normed_mid, up_grad)
    mid_normed_grad = lax.psum(
        matmul_right_t(gate_grad, feed_gate) + matmul_right_t(up_grad, feed_up), "head"
    )
    grad_feed_gain = jnp.sum(mid_normed_grad * middle_normed, axis=0)
    middle_grad = grad_full + norm_back(mid_normed_grad, middle_normed, middle_scale, feed_gain)
    mixer_grad = middle_grad.astype(jnp.bfloat16)
    gated_grad = matmul_right_t(mixer_grad, out_weight)
    grad_out_weight = matmul_back(gated_low, mixer_grad)
    mix_grad, gain_part, gate_proj_grad = gate_back(gated_grad)
    mix_grad_blk = to_blocks(mix_grad.reshape(seq_count, tok_count, head_local, key_size), GROUP)

    def local_pull(carried, pieces):
        query_one, key_one, weight_one, transit_one, grad_one, same_one, enter_one = pieces
        attend = (
            jnp.einsum("shck,shjk->shcj", query_one, key_one, precision=top_precision)
            * same_one
            * causal
        )
        pulled = jnp.einsum("shcj,shcv->shjv", attend, grad_one, precision=top_precision)
        local_term = jnp.einsum(
            "shcv,shck->shvk", enter_one[..., None] * grad_one, query_one, precision=top_precision
        ) - jnp.einsum("shjv,shjk->shvk", pulled, weight_one, precision=top_precision)
        return (local_term + batch_mul(carried, jnp.swapaxes(transit_one, 2, 3)), None)

    local_start, unused_pull = lax.scan(
        local_pull,
        zero_state,
        (query_blk, key_blk, carry_weight, transit, mix_grad_blk, same_blk, enter_blk),
        reverse=True,
    )
    reverse_pair = entering(
        (jnp.swapaxes(device_transit, 2, 3), local_start),
        "seq",
        compose,
        (eye_state, zero_state),
        True,
    )
    summed_grads = read_back((mix_grad, reverse_pair[1]))
    key_prep, value_grad, beta_grad = prep_back(
        (summed_grads[2], summed_grads[3], summed_grads[4], summed_grads[5])
    )
    stacked_grad, edge_grad_local, taps_grad = conv_back(
        (summed_grads[0], summed_grads[1] + key_prep, value_grad)
    )
    edge_from_next = from_behind(edge_grad_local, "seq", -1)
    stacked_grad = stacked_grad + jnp.pad(
        edge_from_next, ((0, 0), (0, 0), (tok_count - delay_rows, 0), (0, 0))
    )
    (logit_grad,) = beta_back(beta_grad)
    query_low = stacked_grad[0].reshape(row_count, channels).astype(jnp.bfloat16)
    key_low = stacked_grad[1].reshape(row_count, channels).astype(jnp.bfloat16)
    value_low = stacked_grad[2].reshape(row_count, channels).astype(jnp.bfloat16)
    gate_low = gate_proj_grad.astype(jnp.bfloat16)
    beta_low = logit_grad.astype(jnp.bfloat16)
    normed_part = (
        matmul_right_t(query_low, query_weight)
        + matmul_right_t(key_low, key_weight)
        + matmul_right_t(value_low, value_weight)
        + matmul_right_t(gate_low, gate_weight)
        + matmul_right_t(beta_low, beta_weight)
    )
    grad_query = matmul_back(normed_in, query_low)
    grad_key = matmul_back(normed_in, key_low)
    grad_value = matmul_back(normed_in, value_low)
    grad_gate = matmul_back(normed_in, gate_low)
    grad_beta = matmul_back(normed_in, beta_low)
    grad_conv = taps_grad.reshape(3, tap_count, head_local, key_size)
    in_normed_grad, head_gain_grad = lax.psum((normed_part, gain_part), "head")
    grad_mixer_gain = jnp.sum(in_normed_grad * input_normed, axis=0)
    input_grad_full = middle_grad + norm_back(in_normed_grad, input_normed, input_scale, mixer_gain)
    input_grad = lax.dynamic_slice_in_dim(
        input_grad_full, lax.axis_index("head") * half_width, half_width, 1
    ).reshape(seq_count, tok_count, half_width)
    all_sums = (
        lax.psum_scatter(grad_mixer_gain, ("dp", "seq"), scatter_dimension=0, tiled=True),
        lax.psum_scatter(grad_query, ("dp", "seq"), scatter_dimension=0, tiled=True),
        lax.psum_scatter(grad_key, ("dp", "seq"), scatter_dimension=0, tiled=True),
        lax.psum_scatter(grad_value, ("dp", "seq"), scatter_dimension=0, tiled=True),
        lax.psum_scatter(grad_gate, ("dp", "seq"), scatter_dimension=0, tiled=True),
        lax.psum_scatter(grad_beta, ("dp", "seq"), scatter_dimension=0, tiled=True),
        lax.psum_scatter(grad_conv, ("dp", "seq"), scatter_dimension=3, tiled=True),
        lax.psum_scatter(head_gain_grad, ("dp", "seq"), scatter_dimension=0, tiled=True),
        lax.psum_scatter(grad_out_weight, ("dp", "seq"), scatter_dimension=1, tiled=True),
        lax.psum_scatter(grad_feed_gain, ("dp", "seq"), scatter_dimension=0, tiled=True),
        lax.psum_scatter(grad_feed_gate, ("dp", "seq"), scatter_dimension=0, tiled=True),
        lax.psum_scatter(grad_feed_up, ("dp", "seq"), scatter_dimension=0, tiled=True),
        lax.psum_scatter(grad_feed_down, ("dp", "seq"), scatter_dimension=1, tiled=True),
    )
    return (
        block_output,
        input_grad,
        all_sums[0],
        all_sums[1],
        all_sums[2],
        all_sums[3],
        all_sums[4],
        all_sums[5],
        all_sums[6],
        all_sums[7],
        all_sums[8],
        all_sums[9],
        all_sums[10],
        all_sums[11],
        all_sums[12],
    )


def solution(mesh):
    return jax.shard_map(
        local,
        mesh=mesh,
        in_specs=(
            P("dp", "seq", "head"),
            P("dp", "seq"),
            P(),
            P(None, "head"),
            P(None, "head"),
            P(None, "head"),
            P(None, "head"),
            P(None, "head"),
            P(None, None, "head", None),
            P(),
            P("head", None),
            P(),
            P(None, "head"),
            P(None, "head"),
            P("head", None),
            P("dp", "seq", "head"),
        ),
        out_specs=(
            P("dp", "seq", "head"),
            P("dp", "seq", "head"),
            P(("dp", "seq")),
            P(("dp", "seq"), "head"),
            P(("dp", "seq"), "head"),
            P(("dp", "seq"), "head"),
            P(("dp", "seq"), "head"),
            P(("dp", "seq"), "head"),
            P(None, None, "head", ("dp", "seq")),
            P(("dp", "seq")),
            P("head", ("dp", "seq")),
            P(("dp", "seq")),
            P(("dp", "seq"), "head"),
            P(("dp", "seq"), "head"),
            P("head", ("dp", "seq")),
        ),
        check_vma=False,
    )
```

profile of v0, /device:TPU:0, one launch (start us, length us, event | category | flops | bytes accessed | tf_op | source)
XLA Modules:
  0.0 1668.4 jit_solution(11679697083530344999)
XLA Ops:
  8.2 5.0 collective-permute-start
  18.8 5.4 all-gather.12.cloned.1.call-done
  70.1 158.9 %custom-call.10 = f32[4,2,4,1,64,64]{4,5,3,2,1,0:T(8,128)} custom-call(f32[4,2,4,1,64,64]{5,4,3,2,1,0:T(8,128)} %add_bitcast_fusion.1), custom_call_target="InvertDiagBlocksLowerTriangular" | custom-call | tf_op jit(solution)/shard_map/jvp(jit(_solve_triangular))/vmap(vmap(vmap()))/triangular_solve | solution.py:210
  232.8 4.9 fusion.189
  237.8 5.0 convolution_subtract_fusion.2
  246.5 28.8 %while.108 = (s32[]{:T(128)}, f32[2,4,128,128]{2,3,1,0:T(8,128)}, f32[2,4,128,128]{2,3,1,0:T(8,128)}, f32[4,2,4,128,128]{3,4,2,1,0:T(8,128)}, f32[4,2,4,128,128]{3,4,2,1,0:T(8,128)}, /*index=5*/s32[]{:T(128)}, s32[]{:T(128)}) while((s32[]{:T(128)}, f32[2,4,128,128]{2,3,1,0:T(8,128)}, f32[2,4,128,128]{2,3,1,0:T(8,128)}, ...), condition=%wide.region_3.4_spmd.clone, body=%wide.region_2.3_spmd.clone.sunk | while | flops 402915328 | bytes 7865982 | solution.py:233
  295.4 17.8 %all-gather.18.cloned.1.call-done = f32[8,4,128,128]{3,2,1,0:T(8,128)} async-done(((f32[2,4,128,128]{3,2,1,0:T(8,128)}), f32[8,4,128,128]{3,2,1,0:T(8,128)}) %all-gather.18.cloned.1.call-update) | async-done | bytes 2097168 | tf_op jit(solution)/shard_map/all_gather | solution.py:24
  313.2 37.2 %all-gather.20.cloned.1.call-done = f32[8,4,128,128]{3,2,1,0:T(8,128)} async-done(((f32[2,4,128,128]{3,2,1,0:T(8,128)}), f32[8,4,128,128]{3,2,1,0:T(8,128)}) %all-gather.20.cloned.1.call-update) | async-done | bytes 2097168 | tf_op jit(solution)/shard_map/all_gather | solution.py:24
  350.3 32.7 %while.109 = (s32[]{:T(128)}, f32[2,4,128,128]{2,3,1,0:T(8,128)}, s32[]{:T(128)}, f32[4,2,4,128,128]{4,3,2,1,0:T(8,128)}, f32[4,2,4,128,128]{4,3,2,1,0:T(8,128)}, /*index=5*/s32[]{:T(128)}, s32[]{:T(128)}) while((s32[]{:T(128)}, f32[2,4,128,128]{2,3,1,0:T(8,128)}, s32[]{:T(128)}, f32[4,2,4,128,128]{4,3,2,1,0:T(8,128)}, ...), condition=%wide.region_5.6_spmd.clone, body=%wide.region_4.5_spmd.clone.sunk | while | flops 201850880 | bytes 5769323 | solution.py:37
  386.8 39.4 %while.106 = (s32[]{:T(128)}, f32[2,4,128,128]{2,3,1,0:T(8,128)S(1)}, f32[4,2,4,64,128]{4,3,0,1,2:T(8,128)}, f32[4,2,4,128,128]{3,4,2,1,0:T(8,128)}, f32[4,2,1,6...) while((s32[]{:T(128)}, ...), condition=%wide.region_8.9_spmd.clone, body=%wide.region_7.8_spmd.clone.sunk | while | flops 503717888 | bytes 13557457 | solution.py:266
  439.3 9.1 reduce-scatter.15.cloned.1.call-done
  451.4 10.3 all-gather.16.cloned.1.call-done
  464.4 10.5 all-gather.14.cloned.1.call-done
  492.6 21.5 %all-reduce.22.cloned.1.call-done = f32[512,1024]{1,0:T(8,128)} async-done(((f32[512,1024]{1,0:T(8,128)}), f32[512,1024]{1,0:T(8,128)}) %all-reduce.22.cloned.1.call-update) | async-done | bytes 2097168 | tf_op jit(solution)/shard_map/psum | solution.py:311
  530.3 48.6 %while.110 = (s32[]{:T(128)}, f32[2,4,128,128]{3,2,1,0:T(8,128)}, f32[4,2,1,64]{3,1,2,0:T(2,128)S(1)}, f32[4,2,4,64,128]{4,3,2,1,0:T(8,128)}, f32[4,2,4,64,128]{...) while((s32[]{:T(128)}, f32[2,4,128,128]{3,2,1,0:T(8,128)}, ...), condition=%wide.region_17.18_spmd.clone, body=%wide.region_16.17_spmd.clone.sunk | while | flops 503848960 | bytes 9309891 | solution.py:335
  579.2 4.5 fusion.234
  587.2 28.5 %all-gather.24.cloned.1.call-done = f32[8,4,128,128]{3,2,1,0:T(8,128)} async-done(((f32[2,4,128,128]{3,2,1,0:T(8,128)}), f32[8,4,128,128]{3,2,1,0:T(8,128)}) %all-gather.24.cloned.1.call-update) | async-done | bytes 2097168 | tf_op jit(solution)/shard_map/all_gather | solution.py:24
  615.6 13.8 while.111
  637.0 78.7 %while.107 = (s32[]{:T(128)}, f32[2,4,128,128]{2,3,1,0:T(8,128)S(1)}, f32[4,2,4,64,128]{4,3,0,2,1:T(8,128)}, f32[4,2,4,64,128]{4,3,2,1,0:T(8,128)}, f32[4,2,4,64...) while((s32[]{:T(128)}, ...), condition=%wide.region_21.22_spmd.clone, body=%wide.region_20.21_spmd.clone.sunk | while | flops 1007296512 | bytes 21425912 | solution.py:266
  719.9 4.3 fusion.145
  728.4 5.2 fusion.222
  788.3 5.8 fusion.244
  794.2 5.7 fusion.245
  814.7 75.3 %all-reduce.18 = (f32[1024]{0:T(1024)S(1)}, f32[3,4,4,128]{3,2,1,0:T(4,128)S(1)}, f32[128]{0:T(128)S(1)}, f32[1024]{0:T(1024)S(1)}) all-reduce(f32[1024]{0:T(1024)S(1)} %get-tuple-element.1410, f32[3,4,4,128]{3,2,1,0:T(4,128)S(1)} %reshape.520, ...), channel_id=8, replica_groups=mesh['dp'=4,'seq'=4,'head'=2] {'dp','seq'}, use_global_device_ids=true, to_apply=%region_30.31.clone | all-reduce | flops 8320 | bytes 66560
  899.6 53.2 %reduce-scatter.25.cloned.1.call-done = f32[64,512]{1,0:T(8,128)} async-done(((f32[1024,512]{1,0:T(8,128)}), f32[64,512]{1,0:T(8,128)}) %reduce-scatter.25.cloned.1.call-update) | async-done | bytes 131088 | tf_op jit(solution)/shard_map/reduce_scatter | solution.py:389
  952.7 80.7 %reduce-scatter.27.cloned.1.call-done = f32[512,64]{0,1:T(8,128)} async-done(((f32[512,1024]{0,1:T(8,128)}), f32[512,64]{0,1:T(8,128)}) %reduce-scatter.27.cloned.1.call-update) | async-done | bytes 131088 | tf_op jit(solution)/shard_map/reduce_scatter | solution.py:393
  1033.5 80.9 %reduce-scatter.19.cloned.1.call-done = f32[64,512]{1,0:T(8,128)} async-done(((f32[1024,512]{1,0:T(8,128)}), f32[64,512]{1,0:T(8,128)}) %reduce-scatter.19.cloned.1.call-update) | async-done | bytes 131088 | tf_op jit(solution)/shard_map/reduce_scatter | solution.py:386
  1114.4 80.4 %reduce-scatter.21.cloned.1.call-done = f32[64,512]{1,0:T(8,128)} async-done(((f32[1024,512]{1,0:T(8,128)}), f32[64,512]{1,0:T(8,128)}) %reduce-scatter.21.cloned.1.call-update) | async-done | bytes 131088 | tf_op jit(solution)/shard_map/reduce_scatter | solution.py:387
  1194.7 80.6 %reduce-scatter.23.cloned.1.call-done = f32[64,512]{1,0:T(8,128)} async-done(((f32[1024,512]{1,0:T(8,128)}), f32[64,512]{1,0:T(8,128)}) %reduce-scatter.23.cloned.1.call-update) | async-done | bytes 131088 | tf_op jit(solution)/shard_map/reduce_scatter | solution.py:388
  1275.3 126.2 %reduce-scatter.29.cloned.1.call-done = f32[64,1408]{1,0:T(8,128)} async-done(((f32[1024,1408]{1,0:T(8,128)}), f32[64,1408]{1,0:T(8,128)}) %reduce-scatter.29.cloned.1.call-update) | async-done | bytes 360464 | tf_op jit(solution)/shard_map/reduce_scatter | solution.py:395
  1401.5 130.0 %reduce-scatter.31.cloned.1.call-done = f32[64,1408]{1,0:T(8,128)} async-done(((f32[1024,1408]{1,0:T(8,128)}), f32[64,1408]{1,0:T(8,128)}) %reduce-scatter.31.cloned.1.call-update) | async-done | bytes 360464 | tf_op jit(solution)/shard_map/reduce_scatter | solution.py:396
  1531.5 129.9 %reduce-scatter.33.cloned.1.call-done = f32[1408,64]{0,1:T(8,128)} async-done(((f32[1408,1024]{0,1:T(8,128)}), f32[1408,64]{0,1:T(8,128)}) %reduce-scatter.33.cloned.1.call-update) | async-done | bytes 360464 | tf_op jit(solution)/shard_map/reduce_scatter | solution.py:397
  (683 shorter events, 473.3 us)
Async XLA Ops:
  7.2 475.6 %copy-start = (bf16[1408,1024]{1,0:T(8,128)(2,1)S(1)}, bf16[1408,1024]{1,0:T(8,128)(2,1)}, u32[]{:S(2)}) copy-start(bf16[1408,1024]{1,0:T(8,128)(2,1)} %param.42) | copy-start | bytes 8650756
  7.2 17.0 %all-gather.12.cloned.1.call-start = ((), (), s32[]{:S(2)}) async-start(), calls=%async_computation.11 | async-start | bytes 3145728 | tf_op jit(solution)/shard_map/all_gather | solution.py:132
  8.2 8.7 collective-permute-start
  13.1 300.0 %all-gather.18.cloned.1.call-start = ((), (), s32[]{:S(2)}) async-start(), calls=%async_computation.26 | async-start | bytes 2621440 | tf_op jit(solution)/shard_map/all_gather | solution.py:24
  14.3 27.5 %copy-start.105 = (f32[2,256]{1,0:T(2,128)}, f32[2,256]{1,0:T(2,128)S(1)}, u32[]{:S(2)}) copy-start(f32[2,256]{1,0:T(2,128)S(1)} %compare_convert_fusion.4) | copy-start | bytes 6148
  15.2 26.6 %copy-start.82 = (f32[3,512]{1,0:T(4,128)}, f32[3,512]{1,0:T(4,128)S(1)}, u32[]{:S(2)}) copy-start(f32[3,512]{1,0:T(4,128)S(1)} %get-tuple-element.1577) | copy-start | bytes 18436
  15.3 26.6 %copy-start.84 = (f32[3,512]{1,0:T(4,128)}, f32[3,512]{1,0:T(4,128)S(1)}, u32[]{:S(2)}) copy-start(f32[3,512]{1,0:T(4,128)S(1)} %get-tuple-element.1578) | copy-start | bytes 18436
  32.6 6.7 collective-permute-start.1
  60.6 228.0 %copy-start.7 = (bf16[4,2,4,64,128]{4,3,2,1,0:T(8,128)(2,1)}, bf16[4,2,4,64,128]{4,3,2,1,0:T(8,128)(2,1)S(1)}, u32[]{:S(2)}) copy-start(bf16[4,2,4,64,128]{4,3,2,1,0:T(8,128)(2,1)S(1)} %fusion.196) | copy-start | bytes 1572868
  277.3 73.0 %all-gather.20.cloned.1.call-start = ((), (), s32[]{:S(2)}) async-start(), calls=%async_computation.27 | async-start | bytes 2621440 | tf_op jit(solution)/shard_map/all_gather | solution.py:24
  279.5 168.9 %reduce-scatter.15.cloned.1.call-start = ((), (), s32[]{:S(2)}) async-start(), calls=%async_computation.12 | async-start | bytes 3145728 | tf_op jit(solution)/shard_map/reduce_scatter | solution.py:285
  438.6 23.0 %all-gather.16.cloned.1.call-start = ((), (), s32[]{:S(2)}) async-start(), calls=%async_computation.15 | async-start | bytes 3145728 | tf_op jit(solution)/shard_map/all_gather | solution.py:301
  439.2 35.7 %all-gather.14.cloned.1.call-start = ((), (), s32[]{:S(2)}) async-start(), calls=%async_computation.13 | async-start | bytes 3145728 | tf_op jit(solution)/shard_map/all_gather | solution.py:287
  451.1 63.0 %all-reduce.22.cloned.1.call-start = ((), (), s32[]{:S(2)}) async-start(), calls=%async_computation.16 | async-start | bytes 4194304 | tf_op jit(solution)/shard_map/psum | solution.py:311
  491.6 95.6 %all-gather.22.cloned.1.call-start = ((), (), s32[]{:S(2)}) async-start(), calls=%async_computation.28 | async-start | bytes 2621440 | tf_op jit(solution)/shard_map/all_gather | solution.py:24
  492.3 123.3 %all-gather.24.cloned.1.call-start = ((), (), s32[]{:S(2)}) async-start(), calls=%async_computation.29 | async-start | bytes 2621440 | tf_op jit(solution)/shard_map/all_gather | solution.py:24
  530.3 48.7 %copy-start.114 = (f32[3,2]{0,1:T(2,128)S(1)}, f32[3,2]{0,1:T(2,128)}, u32[]{:S(2)}) copy-start(f32[3,2]{0,1:T(2,128)} %copy-done.113) | copy-start | bytes 76
  530.3 48.7 %copy-start.116 = (f32[1,2]{0,1:T(2,128)S(1)}, f32[1,2]{0,1:T(2,128)}, u32[]{:S(2)}) copy-start(f32[1,2]{0,1:T(2,128)} %copy-done.115) | copy-start | bytes 28
  578.9 229.5 %reduce-scatter.17.cloned.1.call-start = ((), (), s32[]{:S(2)}) async-start(), calls=%async_computation.14 | async-start | bytes 3145728 | tf_op jit(solution)/shard_map/reduce_scatter | solution.py:298
  583.7 227.5 %all-reduce.24.cloned.1.call-start = ((), (), s32[]{:S(2)}) async-start(), calls=%async_computation.17 | async-start | bytes 4194304 | tf_op jit(solution)/shard_map/psum | solution.py:378
  637.0 78.7 %copy-start.8 = (bf16[4,2,4,64,128]{4,3,2,1,0:T(8,128)(2,1)S(1)}, bf16[4,2,4,64,128]{4,3,2,1,0:T(8,128)(2,1)}, u32[]{:S(2)}) copy-start(bf16[4,2,4,64,128]{4,3,2,1,0:T(8,128)(2,1)} %copy-done.7) | copy-start | bytes 1572868
  758.0 6.0 collective-permute-start.2
  770.9 119.3 %reduce-scatter.35.cloned.1.call-start = ((), (), s32[]{:S(2)}) async-start(), calls=%async_computation.30 | async-start | bytes 557056
  774.4 178.4 %reduce-scatter.25.cloned.1.call-start = ((), (), s32[]{:S(2)}) async-start(), calls=%async_computation.21 | async-start | bytes 2228224 | tf_op jit(solution)/shard_map/reduce_scatter | solution.py:389
  776.6 256.9 %reduce-scatter.27.cloned.1.call-start = ((), (), s32[]{:S(2)}) async-start(), calls=%async_computation.22 | async-start | bytes 2228224 | tf_op jit(solution)/shard_map/reduce_scatter | solution.py:393
  780.8 333.6 %reduce-scatter.19.cloned.1.call-start = ((), (), s32[]{:S(2)}) async-start(), calls=%async_computation.18 | async-start | bytes 2228224 | tf_op jit(solution)/shard_map/reduce_scatter | solution.py:386
  783.9 410.8 %reduce-scatter.21.cloned.1.call-start = ((), (), s32[]{:S(2)}) async-start(), calls=%async_computation.19 | async-start | bytes 2228224 | tf_op jit(solution)/shard_map/reduce_scatter | solution.py:387
  786.1 489.2 %reduce-scatter.23.cloned.1.call-start = ((), (), s32[]{:S(2)}) async-start(), calls=%async_computation.20 | async-start | bytes 2228224 | tf_op jit(solution)/shard_map/reduce_scatter | solution.py:388
  788.3 613.2 %reduce-scatter.29.cloned.1.call-start = ((), (), s32[]{:S(2)}) async-start(), calls=%async_computation.23 | async-start | bytes 6127616 | tf_op jit(solution)/shard_map/reduce_scatter | solution.py:395
  794.1 737.3 %reduce-scatter.31.cloned.1.call-start = ((), (), s32[]{:S(2)}) async-start(), calls=%async_computation.24 | async-start | bytes 6127616 | tf_op jit(solution)/shard_map/reduce_scatter | solution.py:396
  799.9 861.4 %reduce-scatter.33.cloned.1.call-start = ((), (), s32[]{:S(2)}) async-start(), calls=%async_computation.25 | async-start | bytes 6127616 | tf_op jit(solution)/shard_map/reduce_scatter | solution.py:397
  896.3 765.0 %copy-start.1 = (bf16[1408,1024]{1,0:T(8,128)(2,1)S(1)}, bf16[1408,1024]{1,0:T(8,128)(2,1)}, u32[]{:S(2)}) copy-start(bf16[1408,1024]{1,0:T(8,128)(2,1)} %param.42) | copy-start | bytes 8650756
  (125 other events, 513.1 us)
Sparse Core Ops, SparseCore 0:
  13.3 10.8 all-gather.11
  277.5 35.6 all-gather.17
  315.0 35.2 all-gather.19
  438.7 9.5 reduce-scatter.14
  449.8 11.7 all-gather.15
  463.1 11.7 all-gather.13
  491.7 22.3 all-reduce.21
  516.0 36.4 all-gather.21
  579.0 36.5 all-gather.23
  617.7 9.5 reduce-scatter.16
  771.0 22.0 all-reduce.23
  795.2 77.7 reduce-scatter.34
  875.9 76.7 reduce-scatter.24
  955.5 77.8 reduce-scatter.26
  1036.3 78.0 reduce-scatter.18
  1117.2 77.5 reduce-scatter.20
  1197.5 77.7 reduce-scatter.22
  1278.1 123.2 reduce-scatter.28
  1404.5 126.9 reduce-scatter.30
  1534.3 126.9 reduce-scatter.32
where the time goes:
time: 1680 us; the launch traced here: 1670 us
  waiting for transfers between devices  906 us (54%)
  matrix products  291 us (17%)
  other arithmetic  226 us (13%)
  local copies, waits for them, and re-layouts  138 us (8%)
  blocking collectives  78.3 us (5%)
  between operations  17.5 us (1%)
    another operation x5, other arithmetic, block_prep(): jax.scipy.linalg.solve_triangular(system, right_side, lower=True, unit_di...  161 us
    reduce_scatter x1, waiting for transfers between devices, local(): lax.psum_scatter(grad_feed_up, ('dp', 'seq'), scatter_dimension=0, tiled=...  130 us
    reduce_scatter x1, waiting for transfers between devices, local(): lax.psum_scatter(grad_feed_down, ('dp', 'seq'), scatter_dimension=1, tile...  130 us
    reduce_scatter x1, waiting for transfers between devices, local(): lax.psum_scatter(grad_feed_gate, ('dp', 'seq'), scatter_dimension=0, tile...  126 us
    all_gather x4, waiting for transfers between devices, entering(): everything = jax.tree.map(lambda part: lax.all_gather(part, axis), value)  83.4 us
    reduce_scatter x1, waiting for transfers between devices, local(): lax.psum_scatter(grad_query, ('dp', 'seq'), scatter_dimension=0, tiled=True)  80.9 us
    dot_general x32, matrix products, batch_mul(): jnp.einsum('...ij,...jk->...ik', first_op, second_op, precision=top_preci...  80.8 us
    reduce_scatter x1, waiting for transfers between devices, local(): lax.psum_scatter(grad_out_weight, ('dp', 'seq'), scatter_dimension=1, til...  80.7 us
  transfers between devices with their start and end apart: 23, of which 17 were waited for; matrix products, arithmetic and copies ran while one was open for 17% of the time, Pallas kernels for 0%

commit v1 on v0

v1 whole, which is shorter than its diff:
```python
import functools
import math

import jax
import jax.numpy as jnp
from jax import lax
from jax.experimental import pallas as pl
from jax.experimental.pallas import tpu as pltpu
from jax.sharding import PartitionSpec as P

HALO = 16
LONGEST = 512

norm_eps = 1e-05
unit_eps = 1e-06
f32 = jnp.float32
bf16 = jnp.bfloat16
VMEM_LIMIT = 48 * 1024 * 1024


def nn(a, b):
    return lax.dot_general(a, b, (((1,), (0,)), ((), ())), preferred_element_type=f32)


def nt(a, b):
    return lax.dot_general(a, b, (((1,), (1,)), ((), ())), preferred_element_type=f32)


def tn(a, b):
    return lax.dot_general(a, b, (((0,), (0,)), ((), ())), preferred_element_type=f32)


def split(value):
    high = value.astype(bf16)
    return high, (value - high.astype(f32)).astype(bf16)


def nn3(a, b):
    a_high, a_low = a
    b_high, b_low = b
    return nn(a_high, b_high) + nn(a_high, b_low) + nn(a_low, b_high)


def sigmoid(value):
    return 1.0 / (1.0 + jnp.exp(-value))


def rms_scale(values):
    return lax.rsqrt(jnp.mean(values * values, axis=-1, keepdims=True) + norm_eps)


def norm_back(grad_rows, normed, row_scale, gain_vec):
    grad_hat = grad_rows * gain_vec
    return row_scale * (grad_hat - normed * jnp.mean(grad_hat * normed, axis=-1, keepdims=True))


def grid_of(size):
    row = lax.broadcasted_iota(jnp.int32, (size, size), 0)
    return row, lax.broadcasted_iota(jnp.int32, (size, size), 1)


def unit_inverse(lower, size):
    row, col = grid_of(size)
    apart = row ^ col
    inverse = jnp.where(apart == 0, 1.0, 0.0) - jnp.where(apart == 1, lower, 0.0)
    level = 1
    while (1 << level) < size:
        below = jnp.where((apart >> level) == 1, lower, 0.0)
        inverse_parts = split(inverse)
        inverse = inverse - nn3(inverse_parts, split(nn3(split(below), inverse_parts)))
        level += 1
    return inverse


def conv_taps(proj, seq, taps, kind, info, count):
    rows = []
    for tap in range(4):
        moved = proj[seq, HALO - 3 + tap : HALO - 3 + tap + count, :]
        rows.append(moved if tap == 3 else moved * info[seq, :, tap : tap + 1])
    mixed = rows[0] * taps[kind, 0:1, :]
    for tap in range(1, 4):
        mixed = mixed + rows[tap] * taps[kind, tap : tap + 1, :]
    return rows, mixed


def head_column(table, seq, head):
    lane = lax.broadcasted_iota(jnp.int32, table.shape[1:], 1)
    return jnp.sum(jnp.where(lane == head, table[seq], 0.0), axis=1, keepdims=True)


def forward_kernel(
    seqs, count, size,
    query_in, key_in, value_in, taps, info, seg_row, beta,
    query_out, key_out, value_out, inverse_out, fresh_out, carry_out, local_out, reach_out, state_out, transit_out,
):
    head = pl.program_id(0)
    row, col = grid_of(count)
    scale = 1.0 / math.sqrt(size)
    for seq in range(seqs):
        parts = []
        for kind, proj in enumerate((query_in, key_in, value_in)):
            mixed = conv_taps(proj, seq, taps, kind, info, count)[1]
            parts.append(mixed * sigmoid(mixed))
        query, key, value = parts
        query = query * (lax.rsqrt(jnp.sum(query * query, axis=1, keepdims=True) + unit_eps) * scale)
        key = key * lax.rsqrt(jnp.sum(key * key, axis=1, keepdims=True) + unit_eps)
        query, key, value = query.astype(bf16), key.astype(bf16), value.astype(bf16)
        query_out[seq], key_out[seq], value_out[seq] = query, key, value
        enter, last = info[seq, :, 3:4], info[seq, :, 4:5]
        same = info[seq, :, 5:6] == seg_row[seq]
        beta_col = head_column(beta, seq, head)
        key_full = key.astype(f32)
        lower = jnp.where(same & (row > col), nt(key, key) * beta_col, 0.0)
        inverse = unit_inverse(lower, count)
        inverse_parts = split(inverse)
        inverse_out[0, seq] = inverse_parts[0]
        right = jnp.concatenate([key_full * (beta_col * enter), value.astype(f32) * beta_col], axis=1)
        solved = nn3(inverse_parts, split(right))
        solved_high, solved_low = split(solved)
        key_last = (key_full * last).astype(bf16)
        ends = tn(key_last, solved_high) + tn(key_last, solved_low)
        state_out[seq, 0] = ends[:, size:]
        transit_row, transit_col = grid_of(size)
        eye = jnp.where(transit_row == transit_col, 1.0, 0.0)
        transit_out[seq, 0] = eye * info[seq, count - 1 : count, 3:4] - ends[:, :size]
        attend = jnp.where(same & (row >= col), nt(query, key), 0.0).astype(bf16)
        reads = nn(attend, solved_high)
        local_out[seq] = reads[:, size:]
        reach_out[seq] = (query.astype(f32) * enter - reads[:, :size]).astype(bf16)
        carry_out[seq] = solved_high[:, :size]
        fresh_out[seq] = solved[:, size:]


def pl_forward(proj, taps, info, seg_row, beta, first, heads, seqs, count, size, channels):
    def rows(dtype):
        return jax.ShapeDtypeStruct((seqs, count, heads * size), dtype)

    row_spec = pl.BlockSpec((seqs, count, size), lambda h: (0, 0, h))
    proj_spec = pl.BlockSpec((seqs, count + HALO, size), lambda h: (0, 0, h + first))
    state = jax.ShapeDtypeStruct((seqs, heads, size, size), f32)
    state_spec = pl.BlockSpec((seqs, 1, size, size), lambda h: (0, h, 0, 0))
    flops = heads * seqs * (6 * 14 * count**3 + 16 * count * count * size)
    return pl.pallas_call(
        functools.partial(forward_kernel, seqs, count, size),
        grid=(heads,),
        in_specs=[proj_spec] * 3
        + [
            pl.BlockSpec((3, 4, size), lambda h: (0, 0, h + first)),
            pl.BlockSpec(info.shape, lambda h: (0, 0, 0)),
            pl.BlockSpec(seg_row.shape, lambda h: (0, 0, 0)),
            pl.BlockSpec(beta.shape, lambda h: (0, 0, 0)),
        ],
        out_specs=[row_spec] * 3
        + [pl.BlockSpec((1, seqs, count, count), lambda h: (h, 0, 0, 0))]
        + [row_spec] * 4
        + [state_spec] * 2,
        out_shape=[rows(bf16)] * 3
        + [jax.ShapeDtypeStruct((heads, seqs, count, count), bf16)]
        + [rows(f32), rows(bf16), rows(f32), rows(bf16)]
        + [state] * 2,
        compiler_params=pltpu.CompilerParams(vmem_limit_bytes=VMEM_LIMIT),
        cost_estimate=pl.CostEstimate(flops=flops, bytes_accessed=12 << 20, transcendentals=0),
    )(*proj, taps, info, seg_row, beta)


def arrived(hop_refs, seq):
    states, transits = hop_refs
    total = states[-1][seq, 0]
    for state, transit in zip(states[-2::-1], transits[::-1]):
        total = state[seq, 0] + nn3(split(transit[seq, 0]), split(total))
    return total


def read_kernel(seqs, count, size, heads, hops, *refs):
    states, transits = refs[:hops], refs[hops : 2 * hops - 1]
    local, reach, gate, gain, out_weight, state_out, mix_out, gated_out, part_out, held = refs[2 * hops - 1 :]
    head = pl.program_id(0)
    for seq in range(seqs):
        state = arrived((states, transits), seq)
        state_out[seq, 0] = state
        state_high, state_low = split(state)
        moved = reach[seq]
        mix = local[seq] + nn(moved, state_high) + nn(moved, state_low)
        mix_out[seq] = mix
        gate_now = gate[seq]
        gated = (mix * rms_scale(mix) * gain[...] * (gate_now * sigmoid(gate_now))).astype(bf16)
        gated_out[seq] = gated
        held[head, seq * count : (seq + 1) * count, :] = gated

    @pl.when(head == heads - 1)
    def _():
        rows = jnp.concatenate([held[h] for h in range(heads)], axis=1)
        part_out[...] = nn(rows, out_weight[...])


def pl_read(states, transits, local, reach, gate, gain, out_weight, heads, seqs, count, size, width):
    row_spec = pl.BlockSpec((seqs, count, size), lambda h: (0, 0, h))
    state_spec = pl.BlockSpec((seqs, 1, size, size), lambda h: (0, h, 0, 0))
    hops = len(states)
    return pl.pallas_call(
        functools.partial(read_kernel, seqs, count, size, heads, hops),
        grid=(heads,),
        in_specs=[state_spec] * (2 * hops - 1)
        + [row_spec] * 3
        + [pl.BlockSpec((1, size), lambda h: (0, 0)), pl.BlockSpec((heads * size, width), lambda h: (0, 0))],
        out_specs=[state_spec, row_spec, row_spec, pl.BlockSpec((seqs * count, width), lambda h: (0, 0))],
        out_shape=[
            jax.ShapeDtypeStruct((seqs, heads, size, size), f32),
            jax.ShapeDtypeStruct((seqs, count, heads * size), f32),
            jax.ShapeDtypeStruct((seqs, count, heads * size), bf16),
            jax.ShapeDtypeStruct((seqs * count, width), f32),
        ],
        scratch_shapes=[pltpu.VMEM((heads, seqs * count, size), bf16)],
        compiler_params=pltpu.CompilerParams(vmem_limit_bytes=VMEM_LIMIT),
        cost_estimate=pl.CostEstimate(
            flops=2 * seqs * count * heads * size * (width + 2 * size), bytes_accessed=12 << 20, transcendentals=0
        ),
    )(*states, *transits, local, reach, gate, gain, out_weight)


def gate_back_kernel(seqs, count, size, mixer_grad, out_weight, mix, gate, gain, reach, mix_grad, gate_grad, gain_grad, pull):
    head = pl.program_id(0)

    @pl.when(head == 0)
    def _():
        gain_grad[...] = jnp.zeros_like(gain_grad)

    grads = nt(mixer_grad[...], out_weight[...])
    for seq in range(seqs):
        grad = grads[seq * count : (seq + 1) * count]
        mix_now, gate_now = mix[seq], gate[seq]
        scale = rms_scale(mix_now)
        normed = mix_now * scale
        sig = sigmoid(gate_now)
        gate_silu = gate_now * sig
        with_norm = grad * normed
        gain_grad[...] += jnp.sum((with_norm * gate_silu).reshape(count // 8, 8, size), axis=0)
        gate_grad[seq] = (with_norm * gain[...] * (sig * (1.0 + gate_now * (1.0 - sig)))).astype(bf16)
        normed_grad = grad * gain[...] * gate_silu
        mix_grad_now = scale * (normed_grad - normed * jnp.mean(normed_grad * normed, axis=1, keepdims=True))
        low = mix_grad_now.astype(bf16)
        mix_grad[seq] = low
        pull[seq, 0] = tn(reach[seq], low)


def pl_gate_back(mixer_grad, out_weight, mix, gate, gain, reach, heads, seqs, count, size, width):
    row_spec = pl.BlockSpec((seqs, count, size), lambda h: (0, 0, h))
    return pl.pallas_call(
        functools.partial(gate_back_kernel, seqs, count, size),
        grid=(heads,),
        in_specs=[
            pl.BlockSpec((seqs * count, width), lambda h: (0, 0)),
            pl.BlockSpec((size, width), lambda h: (h, 0)),
            row_spec,
            row_spec,
            pl.BlockSpec((1, size), lambda h: (0, 0)),
            row_spec,
        ],
        out_specs=[
            row_spec,
            row_spec,
            pl.BlockSpec((8, size), lambda h: (0, 0)),
            pl.BlockSpec((seqs, 1, size, size), lambda h: (0, h, 0, 0)),
        ],
        out_shape=[
            jax.ShapeDtypeStruct((seqs, count, heads * size), bf16),
            jax.ShapeDtypeStruct((seqs, count, heads * size), bf16),
            jax.ShapeDtypeStruct((8, size), f32),
            jax.ShapeDtypeStruct((seqs, heads, size, size), f32),
        ],
        compiler_params=pltpu.CompilerParams(vmem_limit_bytes=VMEM_LIMIT),
        cost_estimate=pl.CostEstimate(
            flops=2 * seqs * count * heads * size * (width + size), bytes_accessed=8 << 20, transcendentals=0
        ),
    )(mixer_grad, out_weight, mix, gate, gain, reach)


def backward_kernel(seqs, count, size, hops, *refs):
    pulls, transits = refs[:hops], refs[hops : 2 * hops - 1]
    (
        query_in, key_in, value_in, taps, info, seg_row, beta,
        query_ref, key_ref, value_ref, inverse_ref, fresh_ref, carry_ref, mix_grad_ref, state_ref,
        query_grad_out, key_grad_out, value_grad_out, edge_out, taps_grad_out, logit_grad_out,
    ) = refs[2 * hops - 1 :]
    head = pl.program_id(0)
    row, col = grid_of(count)
    scale = 1.0 / math.sqrt(size)

    @pl.when(head == 0)
    def _():
        logit_grad_out[...] = jnp.zeros_like(logit_grad_out)

    taps_totals = None
    for seq in range(seqs):
        total = pulls[-1][seq, 0]
        for pull, transit in zip(pulls[-2::-1], transits[::-1]):
            transit_high, transit_low = split(transit[seq, 0])
            total_high, total_low = split(total)
            total = pull[seq, 0] + (
                tn(transit_high, total_high) + tn(transit_high, total_low) + tn(transit_low, total_high)
            )
        out_state_grad = total.astype(bf16)
        state = state_ref[seq, 0].astype(bf16)
        query, key, value = query_ref[seq], key_ref[seq], value_ref[seq]
        mix_grad = mix_grad_ref[seq]
        enter, last = info[seq, :, 3:4], info[seq, :, 4:5]
        same = info[seq, :, 5:6] == seg_row[seq]
        causal = same & (row >= col)
        strict = same & (row > col)
        beta_col = head_column(beta, seq, head)
        key_full = key.astype(f32)
        key_last = (key_full * last).astype(bf16)
        update = (fresh_ref[seq] - nn(carry_ref[seq], state)).astype(bf16)
        attend = jnp.where(causal, nt(query, key), 0.0).astype(bf16)
        update_grad = tn(attend, mix_grad) + nn(key_last, out_state_grad)
        right_grad = tn(inverse_ref[0, seq], update_grad.astype(bf16))
        right_low = right_grad.astype(bf16)
        both = nt(jnp.concatenate([mix_grad, right_low], axis=0), update)
        attend_grad = jnp.where(causal, both[:count], 0.0).astype(bf16)
        lower_grad = jnp.where(strict, -both[count:], 0.0)
        gram = nt(key, key)
        surprise = value.astype(f32) - enter * nn(key, state)
        beta_grad = jnp.sum(right_grad * surprise, axis=1, keepdims=True) + jnp.sum(
            lower_grad * gram, axis=1, keepdims=True
        )
        logit_grad = beta_grad * beta_col * (1.0 - beta_col)
        lane = lax.broadcasted_iota(jnp.int32, logit_grad_out.shape[1:], 1)
        logit_grad_out[seq] += jnp.where(lane == head, logit_grad, 0.0)
        value_grad = right_grad * beta_col
        gram_grad = (lower_grad * beta_col).astype(bf16)
        stacked = jnp.concatenate([gram_grad, attend_grad], axis=0)
        forth = nn(stacked, key)
        back = tn(stacked, jnp.concatenate([key, query], axis=0))
        through = nt(
            jnp.concatenate([(value_grad * enter).astype(bf16), mix_grad], axis=0), state
        )
        key_grad = forth[:count] + back - through[:count] + last * nt(update, out_state_grad)
        query_grad = forth[count:] + enter * through[count:]
        for kind, (proj, grad, out) in enumerate(
            (
                (query_in, query_grad, query_grad_out),
                (key_in, key_grad, key_grad_out),
                (value_in, value_grad, value_grad_out),
            )
        ):
            rows, mixed = conv_taps(proj, seq, taps, kind, info, count)
            sig = sigmoid(mixed)
            if kind < 2:
                active = mixed * sig
                norm = lax.rsqrt(jnp.sum(active * active, axis=1, keepdims=True) + unit_eps)
                unit = active * norm
                grad = grad - unit * jnp.sum(grad * unit, axis=1, keepdims=True)
                grad = grad * (norm * scale if kind == 0 else norm)
            mixed_grad = grad * (sig * (1.0 + mixed * (1.0 - sig)))
            sums = [jnp.sum((mixed_grad * rows[tap]).reshape(count // 8, 8, size), axis=0) for tap in range(4)]
            blank = jnp.zeros((8, size), f32)
            proj_grad = mixed_grad * taps[kind, 3:4, :]
            edge = blank
            for tap in range(3):
                delay = 3 - tap
                masked = mixed_grad * (info[seq, :, tap : tap + 1] * taps[kind, tap : tap + 1, :])
                moved = pltpu.roll(masked, count - delay, 0)
                at = lax.broadcasted_iota(jnp.int32, (count, size), 0)
                proj_grad = proj_grad + jnp.where(at < count - delay, moved, 0.0)
                first = pltpu.roll(masked[:8], 8 - delay, 0)
                at_edge = lax.broadcasted_iota(jnp.int32, (8, size), 0)
                edge = edge + jnp.where(at_edge >= 8 - delay, first, 0.0)
            out[seq] = proj_grad
            edge_out[kind, seq] = edge
            sums = jnp.stack([jnp.sum(part, axis=0) for part in sums])
            if seq == 0:
                taps_grad_out[kind] = sums
            else:
                taps_grad_out[kind] += sums


def pl_backward(pulls, transits, proj, taps, info, seg_row, beta, saved, mix_grad, state, heads, seqs, count, size):
    hops = len(pulls)
    row_spec = pl.BlockSpec((seqs, count, size), lambda h: (0, 0, h))
    state_spec = pl.BlockSpec((seqs, 1, size, size), lambda h: (0, h, 0, 0))
    proj_spec = pl.BlockSpec((seqs, count + HALO, size), lambda h: (0, 0, h))
    flops = heads * seqs * 2 * count * count * size * 16
    return pl.pallas_call(
        functools.partial(backward_kernel, seqs, count, size, hops),
        grid=(heads,),
        in_specs=[state_spec] * (2 * hops - 1)
        + [proj_spec] * 3
        + [
            pl.BlockSpec((3, 4, size), lambda h: (0, 0, h)),
            pl.BlockSpec(info.shape, lambda h: (0, 0, 0)),
            pl.BlockSpec(seg_row.shape, lambda h: (0, 0, 0)),
            pl.BlockSpec(beta.shape, lambda h: (0, 0, 0)),
        ]
        + [row_spec] * 3
        + [pl.BlockSpec((1, seqs, count, count), lambda h: (h, 0, 0, 0))]
        + [row_spec] * 3
        + [state_spec],
        out_specs=[row_spec] * 3
        + [
            pl.BlockSpec((3, seqs, 8, size), lambda h: (0, 0, 0, h)),
            pl.BlockSpec((3, 4, size), lambda h: (0, 0, h)),
            pl.BlockSpec((seqs, count, heads), lambda h: (0, 0, 0)),
        ],
        out_shape=[jax.ShapeDtypeStruct((seqs, count, heads * size), f32)] * 3
        + [
            jax.ShapeDtypeStruct((3, seqs, 8, heads * size), f32),
            jax.ShapeDtypeStruct((3, 4, heads * size), f32),
            jax.ShapeDtypeStruct((seqs, count, heads), f32),
        ],
        compiler_params=pltpu.CompilerParams(vmem_limit_bytes=VMEM_LIMIT),
        cost_estimate=pl.CostEstimate(flops=flops, bytes_accessed=16 << 20, transcendentals=0),
    )(*pulls, *transits, *proj, taps, info, seg_row, beta, *saved, mix_grad, state)


def shifted(value, axis, steps):
    count = lax.axis_size(axis)
    initial, last = (max(0, -steps), min(count, count - steps))
    return lax.ppermute(value, axis, [(source, source + steps) for source in range(initial, last)])


def swapped(value):
    return lax.ppermute(value, "head", [(0, 1), (1, 0)])


def in_order(own, other, axis):
    mine = lax.axis_index("head") == 0
    return jnp.where(
        mine, jnp.concatenate([own, other], axis=axis), jnp.concatenate([other, own], axis=axis)
    )


def own_half(value, half):
    return lax.dynamic_slice_in_dim(value, lax.axis_index("head") * half, half, value.ndim - 1)


def pick(value, index, axis):
    return lax.dynamic_index_in_dim(value, index, axis, keepdims=False)


def scatter_sum(first, second):
    dp, seq = lax.axis_size("dp"), lax.axis_size("seq")
    rows = first.shape[0]
    if seq != 4:
        return tuple(
            lax.psum_scatter(part, ("dp", "seq"), scatter_dimension=0, tiled=True) for part in (first, second)
        )
    place = lax.axis_index("seq")
    low, high = place % 2, place // 2
    across_low = [(source, source ^ 1) for source in range(4)]
    across_high = [(source, source ^ 2) for source in range(4)]
    first = first.reshape(dp, 2, 2, rows // (4 * dp), first.shape[1])
    second = second.reshape(dp, 2, 2, rows // (4 * dp), second.shape[1])
    first_in = lax.ppermute(pick(first, 1 - low, 2), "seq", across_low)
    second_in = lax.ppermute(pick(second, 1 - high, 1), "seq", across_high)
    first = pick(first, low, 2) + first_in
    second = pick(second, high, 1) + second_in
    first_in = lax.ppermute(pick(first, 1 - high, 1), "seq", across_high)
    second_in = lax.ppermute(pick(second, 1 - low, 1), "seq", across_low)
    first = pick(first, high, 1) + first_in
    second = pick(second, low, 1) + second_in
    cut = first.shape[-1]
    joined = jnp.concatenate([first, second], axis=-1).reshape(rows // 4, -1)
    joined = lax.psum_scatter(joined, "dp", scatter_dimension=0, tiled=True)
    return joined[:, :cut], joined[:, cut:]


def local(
    block_input,
    segment_ids,
    mixer_gain,
    query_weight,
    key_weight,
    value_weight,
    gate_weight,
    beta_weight,
    conv_weight,
    head_gain,
    out_weight,
    feed_gain,
    feed_gate,
    feed_up,
    feed_down,
    grad_output,
):
    seqs, count, half = block_input.shape
    rows = seqs * count
    size = head_gain.shape[0]
    heads = beta_weight.shape[1]
    channels = heads * size
    width = query_weight.shape[0]
    hops = -(-(LONGEST - 1) // count)
    hops = min(hops, lax.axis_size("seq") - 1)

    other_input = swapped(block_input)
    before = shifted(block_input[:, count - 3 :], "seq", 1)
    other_before = swapped(before)
    full_input = in_order(block_input, other_input, 2)
    full_before = in_order(before, other_before, 2)
    segments = segment_ids.astype(f32)
    edge_ids = shifted(segments[:, count - 3 :], "seq", 1)
    other_grad = swapped(grad_output)

    extended = jnp.concatenate(
        [jnp.zeros((seqs, HALO - 3, width), f32), full_before, full_input], axis=1
    )
    extended_low = (extended * rms_scale(extended) * mixer_gain).astype(bf16)
    flat = extended_low.reshape(seqs * (count + HALO), width)
    proj = [
        nn(flat, weight).reshape(seqs, count + HALO, channels)
        for weight in (query_weight, key_weight, value_weight)
    ]
    normed_in = extended_low[:, HALO:].reshape(rows, width)
    beta = jax.nn.sigmoid(nn(normed_in, beta_weight)).reshape(seqs, count, heads)
    gate_proj = nn(normed_in, gate_weight).reshape(seqs, count, channels)

    extended_ids = jnp.concatenate([edge_ids, segments], axis=1)
    masks = [(extended_ids[:, tap : tap + count] == segments) for tap in range(3)]
    enter = segments == edge_ids[:, 2:3]
    last = segments == segments[:, count - 1 :]
    zero = jnp.zeros_like(segments)
    info = jnp.stack(
        [mask.astype(f32) for mask in masks] + [enter.astype(f32), last.astype(f32), segments, zero, zero], axis=-1
    )
    seg_row = segments[:, None, :]
    taps = conv_weight.reshape(3, 4, channels)
    gain = head_gain[None, :]

    (query, key, value, inverse, fresh, carry, local_mix, reach, state_end, transit) = pl_forward(
        proj, taps, info, seg_row, beta, 0, heads, seqs, count, size, channels
    )
    states = [shifted(state_end, "seq", hop) for hop in range(1, hops + 1)]
    transits = [shifted(transit, "seq", hop) for hop in range(1, hops)]
    state, mix, gated, part = pl_read(
        states, transits, local_mix, reach, gate_proj, gain, out_weight, heads, seqs, count, size, width
    )
    gated = gated.reshape(rows, channels)

    flat_input = full_input.reshape(rows, width)
    middle = flat_input + (part + swapped(part))
    middle_scale = rms_scale(middle)
    middle_normed = middle * middle_scale
    normed_mid = (middle_normed * feed_gain).astype(bf16)
    gate_act = nn(normed_mid, feed_gate)
    up_act = nn(normed_mid, feed_up)
    gate_sig = jax.nn.sigmoid(gate_act)
    gate_silu = gate_act * gate_sig
    inner = (gate_silu * up_act).astype(bf16)
    full_grad = in_order(grad_output, other_grad, 2).reshape(rows, width)
    down_grad = full_grad.astype(bf16)
    cut = feed_down.shape[0] // 256 * 128
    sums_down = scatter_sum(tn(down_grad, inner[:, :cut]), tn(down_grad, inner[:, cut:]))
    inner_grad = nt(down_grad, feed_down)
    gate_grad = (inner_grad * up_act * (gate_sig * (1.0 + gate_act * (1.0 - gate_sig)))).astype(bf16)
    up_grad = (inner_grad * gate_silu).astype(bf16)
    sums_feed = scatter_sum(tn(normed_mid, gate_grad), tn(normed_mid, up_grad))
    mid_part = nt(gate_grad, feed_gate) + nt(up_grad, feed_up)
    mid_grad = mid_part + swapped(mid_part)
    grad_feed_gain = jnp.sum(mid_grad * middle_normed, axis=0)
    middle_grad = full_grad + norm_back(mid_grad, middle_normed, middle_scale, feed_gain)
    mixer_grad = middle_grad.astype(bf16)

    down_part = nn(inner, feed_down)
    mine = lax.axis_index("head")
    down_out = lax.dynamic_slice_in_dim(down_part, (1 - mine) * half, half, 1)
    block_output = own_half(middle, half) + (own_half(down_part, half) + swapped(down_out))

    mix_grad, gate_low, gain_grad, pull = pl_gate_back(
        mixer_grad, out_weight, mix, gate_proj, gain, reach, heads, seqs, count, size, width
    )
    gate_low = gate_low.reshape(rows, channels)
    pulls = [shifted(pull, "seq", -hop) for hop in range(1, hops + 1)]
    back_transits = [shifted(transit, "seq", -hop) for hop in range(1, hops)]
    sums_out = scatter_sum(tn(mixer_grad, gated), tn(normed_in, gate_low))
    query_grad, key_grad, value_grad, edge, taps_grad, logit_grad = pl_backward(
        pulls, back_transits, proj, taps, info, seg_row, beta,
        (query, key, value, inverse, fresh, carry), mix_grad, state, heads, seqs, count, size,
    )
    edge = shifted(edge, "seq", -1)
    lows = [
        (grad + jnp.pad(edge[kind], ((0, 0), (count - 8, 0), (0, 0)))).astype(bf16).reshape(rows, channels)
        for kind, grad in enumerate((query_grad, key_grad, value_grad))
    ]
    beta_low = logit_grad.astype(bf16).reshape(rows, heads)
    sums_query = scatter_sum(tn(normed_in, lows[0]), tn(normed_in, lows[1]))
    last_sums = tn(normed_in, lows[2])
    sums_value = scatter_sum(last_sums[:, : channels // 2], last_sums[:, channels // 2 :])
    in_part = (
        nt(lows[0], query_weight)
        + nt(lows[1], key_weight)
        + nt(lows[2], value_weight)
        + nt(gate_low, gate_weight)
        + nt(beta_low, beta_weight)
    )
    in_grad = in_part + swapped(in_part)
    input_scale = rms_scale(flat_input)
    input_normed = flat_input * input_scale
    grad_mixer_gain = jnp.sum(in_grad * input_normed, axis=0)
    input_grad = own_half(middle_grad + norm_back(in_grad, input_normed, input_scale, mixer_gain), half)
    grad_beta = tn(normed_in, beta_low)

    blocks = lax.axis_size("dp") * lax.axis_size("seq")
    head_part = jnp.sum(gain_grad, axis=0)
    head_part = head_part + swapped(head_part)
    pieces = [
        grad_mixer_gain.reshape(blocks, -1),
        grad_feed_gain.reshape(blocks, -1),
        grad_beta.reshape(blocks, -1),
        taps_grad.reshape(12 * heads, blocks, size // blocks).transpose(1, 0, 2).reshape(blocks, -1),
        head_part.reshape(blocks, -1),
    ]
    small = jnp.concatenate(pieces, axis=1)
    small = jnp.pad(small, ((0, 0), (0, -small.shape[1] % 1024)))
    small = lax.psum_scatter(small.reshape(-1, 128), ("dp", "seq"), scatter_dimension=0, tiled=True).reshape(-1)
    cuts, at = [], 0
    for piece in pieces:
        cuts.append(small[at : at + piece.shape[1]])
        at += piece.shape[1]
    shape = (seqs, count, half)
    return (
        block_output.reshape(shape),
        input_grad.reshape(shape),
        cuts[0],
        sums_query[0],
        sums_query[1],
        jnp.concatenate(sums_value, axis=1),
        sums_out[1],
        cuts[2].reshape(-1, heads),
        cuts[3].reshape(3, 4, heads, size // blocks),
        cuts[4],
        sums_out[0].T,
        cuts[1],
        sums_feed[0],
        sums_feed[1],
        jnp.concatenate(sums_down, axis=1).T,
    )


def solution(mesh):
    return jax.shard_map(
        local,
        mesh=mesh,
        in_specs=(
            P("dp", "seq", "head"),
            P("dp", "seq"),
            P(),
            P(None, "head"),
            P(None, "head"),
            P(None, "head"),
            P(None, "head"),
            P(None, "head"),
            P(None, None, "head", None),
            P(),
            P("head", None),
            P(),
            P(None, "head"),
            P(None, "head"),
            P("head", None),
            P("dp", "seq", "head"),
        ),
        out_specs=(
            P("dp", "seq", "head"),
            P("dp", "seq", "head"),
            P(("dp", "seq")),
            P(("dp", "seq"), "head"),
            P(("dp", "seq"), "head"),
            P(("dp", "seq"), "head"),
            P(("dp", "seq"), "head"),
            P(("dp", "seq"), "head"),
            P(None, None, "head", ("dp", "seq")),
            P(("dp", "seq")),
            P("head", ("dp", "seq")),
            P(("dp", "seq")),
            P(("dp", "seq"), "head"),
            P(("dp", "seq"), "head"),
            P("head", ("dp", "seq")),
        ),
        check_vma=False,
    )
```

time: 1680 us -> 574 us (0.34)
  waiting for transfers between devices: 906 us -> 234 us
  matrix products: 291 us -> 43.2 us
  other arithmetic: 226 us -> 63.5 us
  blocking collectives: 78.3 us -> 0 us
  Pallas kernels: 0 us -> 75.2 us
  local copies, waits for them, and re-layouts: 138 us -> 72.7 us
  starting transfers between devices: 12.1 us -> 56.8 us
    reduce_scatter x10 -> x5, waiting for transfers between devices: 771 us -> 31.8 us  [scatter_sum(): joined = lax.psum_scatter(joined, 'dp', scatter_dimension=0, tiled=True)]
    dot_general x132 -> x26, matrix products: 279 us -> 43.2 us  [the longest x10 15.4 us: tn(): lax.dot_general(a, b, (((0,), (0,)), ((), ())), preferred_element_type=f32)]
    ppermute x3 -> x37, waiting for transfers between devices: 2.15 us -> 202 us  [the longest x9 84.8 us: shifted(): lax.ppermute(value, axis, [(source, source + steps) for source in range(i...]
    another operation x7 -> x3, other arithmetic: 162 us -> 1.51 us  [local(): jnp.stack([mask.astype(f32) for mask in masks] + [enter.astype(f32), last...]
    all_gather x7 -> x0, waiting for transfers between devices: 110 us -> none  [the longest x4 83.4 us: entering(): everything = jax.tree.map(lambda part: lax.all_gather(part, axis), value)]
    unnamed x1 -> x0, blocking collectives: 75.3 us -> none
    pallas_call x0 -> x4, Pallas kernels: none -> 75.2 us  [the longest x1 46.3 us: pl_forward(): pl.pallas_call(functools.partial(forward_kernel, seqs, count, size), grid...]
    ppermute x3 -> x37, starting transfers between devices: 10.3 us -> 56.3 us  [the longest x9 23.7 us: shifted(): lax.ppermute(value, axis, [(source, source + steps) for source in range(i...]
  transfers between devices with their start and end apart: 23 -> 43, of which waited for: 17 -> 16; matrix products, arithmetic and copies ran while one was open for 17% -> 24% of each run, Pallas kernels for 0% -> 4%
where the time goes in v1:
time: 574 us; the launch traced here: 564 us
  waiting for transfers between devices  234 us (41%)
  Pallas kernels  75.2 us (13%)
  local copies, waits for them, and re-layouts  72.7 us (13%)
  other arithmetic  63.5 us (11%)
  starting transfers between devices  56.8 us (10%)
  matrix products  43.2 us (8%)
  between operations  18.2 us (3%)
    ppermute x9, waiting for transfers between devices, shifted(): lax.ppermute(value, axis, [(source, source + steps) for source in range(i...  84.8 us
    pallas_call x1, Pallas kernels, pl_forward(): pl.pallas_call(functools.partial(forward_kernel, seqs, count, size), grid...  46.3 us
    ppermute x5, waiting for transfers between devices, scatter_sum(): second_in = lax.ppermute(pick(second, 1 - low, 1), 'seq', across_low)  41.4 us
    reduce_scatter x5, waiting for transfers between devices, scatter_sum(): joined = lax.psum_scatter(joined, 'dp', scatter_dimension=0, tiled=True)  31.8 us
    ppermute x5, waiting for transfers between devices, scatter_sum(): first_in = lax.ppermute(pick(first, 1 - high, 1), 'seq', across_high)  31.2 us
    unnamed x197, local copies, waits for them, and re-layouts  28 us
    ppermute x9, starting transfers between devices, shifted(): lax.ppermute(value, axis, [(source, source + steps) for source in range(i...  23.7 us
    ppermute x5, waiting for transfers between devices, scatter_sum(): first_in = lax.ppermute(pick(first, 1 - low, 2), 'seq', across_low)  23.2 us
  transfers between devices with their start and end apart: 43, of which 16 were waited for; matrix products, arithmetic and copies ran while one was open for 24% of the time, Pallas kernels for 4%

profile of v1, /device:TPU:0, one launch (start us, length us, event | category | flops | bytes accessed | tf_op | source)
XLA Modules:
  0.0 563.7 jit_solution(6819466585097038971)
XLA Ops:
  9.6 4.3 collective-permute-start.1
  14.7 3.4 collective-permute-start.3
  37.9 46.3 %shard_map.271 = (bf16[2,256,512]{2,1,0:T(8,128)(2,1)S(1)}, bf16[2,256,512]{2,1,0:T(8,128)(2,1)S(1)}, bf16[2,256,512]{2,1,0:T(8,128)(2,1)S(1)}, bf16[4,2,256,256...) custom-call(f32[2,272,512]{2,1,0:T(8,128)} %fusion.12.query_in.refs_, ...), custom_call_target="tpu_custom_call" | custom-call | flops 12348030976 | bytes 12582912 | tf_op jit(solution)/shard_map/pallas_call | solution.py:143
  85.2 4.5 collective-permute-start.4
  97.5 4.4 collective-permute-done.4.refs_0_
  101.9 23.9 %collective-permute-done.5.refs_1_ = f32[2,4,128,128]{3,2,1,0:T(8,128)S(1)} collective-permute-done((f32[2,4,128,128]{3,2,1,0:T(8,128)S(1)}, f32[2,4,128,128]{3,2,1,0:T(8,128)S(1)}, u32[]{:S(2)}, u32[]{:S(2)}) %collective-permute-start.5) | collective-permute-done | bytes 524320 | tf_op jit(solution)/shard_map/ppermute | solution.py:418
  125.8 7.0 %shard_map.272 = (f32[2,4,128,128]{3,2,1,0:T(8,128)S(1)}, f32[2,256,512]{2,1,0:T(8,128)S(1)}, bf16[2,256,512]{2,1,0:T(8,128)(2,1)S(1)}, f32[512,1024]{1,0:T(8,128)}) custom-call(f32[2,4,128,128]{3,2,1,0:T(8,128)S(1)} %collective-permute-done.4.refs_0_, f32[2,4,128,128]{3,2,1,0:T(8,128)S(1)} %collective-permute-done.5.refs_1_, ...), custom_call_target="tpu_custom_call" | custom-call | flops 671088640 | bytes 12582912 | tf_op jit(solution)/shard_map/pallas_call | solution.py:200
  133.4 5.4 collective-permute-done.7
  148.2 3.7 multiply_convert_fusion
  160.8 3.5 fusion.47
  179.7 4.5 fusion.29
  184.2 5.5 shard_map.273
  207.0 3.3 collective-permute-start.29
  211.1 3.4 collective-permute-start.27
  215.3 30.7 %collective-permute-done.12.refs_1_ = f32[2,4,128,128]{3,2,1,0:T(8,128)} collective-permute-done((f32[2,4,128,128]{3,2,1,0:T(8,128)}, f32[2,4,128,128]{3,2,1,0:T(8,128)}, u32[]{:S(2)}, u32[]{:S(2)}) %collective-permute-start.12) | collective-permute-done | bytes 524320 | tf_op jit(solution)/shard_map/ppermute | solution.py:418
  252.3 16.4 %shard_map.274 = (f32[2,256,512]{2,1,0:T(8,128)}, f32[2,256,512]{2,1,0:T(8,128)}, f32[2,256,512]{2,1,0:T(8,128)}, f32[3,2,8,512]{3,2,1,0:T(8,128)}, f32[3,4,512]{2,1,0:T(4,128)S(1)}, /*index=5*/f32[2,256,4]{2,1,0:T(8,128)S(1)}) custom-call(f32[2,4,128,128]{3,2,1,0:T(8,128)} %collective-permute-done.11.refs_0_, ...), custom_call_target="tpu_custom_call" | custom-call | flops 2147483648 | bytes 16777216 | tf_op jit(solution)/shard_map/pallas_call | solution.py:383
  272.8 25.6 %collective-permute-done.14 = f32[3,2,8,512]{3,2,1,0:T(8,128)} collective-permute-done((f32[3,2,8,512]{3,2,1,0:T(8,128)}, f32[3,2,8,512]{3,2,1,0:T(8,128)}, u32[]{:S(2)}, u32[]{:S(2)}) %collective-permute-start.14) | collective-permute-done | bytes 98336 | tf_op jit(solution)/shard_map/ppermute | solution.py:418
  311.5 4.0 collective-permute-start.19
  325.6 8.1 %collective-permute-done.28 = f32[4,64,512]{2,1,0:T(8,128)S(1)} collective-permute-done((f32[4,64,512]{2,1,0:T(8,128)S(1)}, f32[4,64,512]{2,1,0:T(8,128)S(1)}, u32[]{:S(2)}, u32[]{:S(2)}) %collective-permute-start.28) | collective-permute-done | bytes 524320 | tf_op jit(solution)/shard_map/ppermute | solution.py:458
  335.6 14.6 %collective-permute-done.26 = f32[4,64,512]{2,1,0:T(8,128)S(1)} collective-permute-done((f32[4,64,512]{2,1,0:T(8,128)S(1)}, f32[4,64,512]{2,1,0:T(8,128)S(1)}, u32[]{:S(2)}, u32[]{:S(2)}) %collective-permute-start.26) | collective-permute-done | bytes 524320 | tf_op jit(solution)/shard_map/ppermute | solution.py:457
  353.5 4.9 multiply_reduce_fusion.2
  372.7 27.7 %collective-permute-done.20 = f32[4,64,512]{2,1,0:T(8,128)S(1)} collective-permute-done((f32[4,64,512]{2,1,0:T(8,128)S(1)}, f32[4,64,512]{2,1,0:T(8,128)S(1)}, u32[]{:S(2)}, u32[]{:S(2)}) %collective-permute-start.20) | collective-permute-done | bytes 524320 | tf_op jit(solution)/shard_map/ppermute | solution.py:458
  403.8 9.7 %collective-permute-done.30 = f32[4,64,1408]{2,1,0:T(8,128)} collective-permute-done((f32[4,64,1408]{2,1,0:T(8,128)}, f32[4,64,1408]{2,1,0:T(8,128)}, u32[]{:S(2)}, u32[]{:S(2)}) %collective-permute-start.30) | collective-permute-done | bytes 1441824 | tf_op jit(solution)/shard_map/ppermute | solution.py:457
  417.2 3.5 fusion.23
  433.3 23.2 %collective-permute-done.33 = f32[4,2,64,640]{3,2,1,0:T(8,128)} collective-permute-done((f32[4,2,64,640]{3,2,1,0:T(8,128)}, f32[4,2,64,640]{3,2,1,0:T(8,128)}, u32[]{:S(2)}, u32[]{:S(2)}) %collective-permute-start.33) | collective-permute-done | bytes 1310752 | tf_op jit(solution)/shard_map/ppermute | solution.py:453
  463.7 6.9 %collective-permute-done.35 = f32[4,2,64,768]{3,2,1,0:T(8,128)} collective-permute-done((f32[4,2,64,768]{3,2,1,0:T(8,128)}, f32[4,2,64,768]{3,2,1,0:T(8,128)}, u32[]{:S(2)}, u32[]{:S(2)}) %collective-permute-start.35) | collective-permute-done | bytes 1572896 | tf_op jit(solution)/shard_map/ppermute | solution.py:454
  472.2 9.5 %collective-permute-done.23 = f32[4,2,64,256]{3,2,1,0:T(8,128)S(1)} collective-permute-done((f32[4,2,64,256]{3,2,1,0:T(8,128)S(1)}, f32[4,2,64,256]{3,2,1,0:T(8,128)S(1)}, u32[]{:S(2)}, u32[]{:S(2)}) %collective-permute-start.23) | collective-permute-done | bytes 524320 | tf_op jit(solution)/shard_map/ppermute | solution.py:454
  485.6 5.6 collective-permute-done.24
  491.2 6.9 %collective-permute-done.22 = f32[4,64,256]{2,1,0:T(8,128)S(1)} collective-permute-done((f32[4,64,256]{2,1,0:T(8,128)S(1)}, f32[4,64,256]{2,1,0:T(8,128)S(1)}, u32[]{:S(2)}, u32[]{:S(2)}) %collective-permute-start.22) | collective-permute-done | bytes 262176 | tf_op jit(solution)/shard_map/ppermute | solution.py:457
  499.1 3.3 fusion.36
  508.7 3.4 add_add_fusion.2
  523.9 31.8 %reduce-scatter.14.cloned.1.call-done = f32[64,1408]{1,0:T(8,128)} async-done(((f32[256,1408]{1,0:T(8,128)}), f32[64,1408]{1,0:T(8,128)}) %reduce-scatter.14.cloned.1.call-update) | async-done | bytes 360464 | tf_op jit(solution)/shard_map/reduce_scatter | solution.py:463
  (402 shorter events, 186.9 us)
Async XLA Ops:
  8.0 506.5 %all-reduce.7.cloned.1.call-start = ((), (), s32[]{:S(2)}) async-start(), calls=%async_computation.10 | async-start | bytes 131072
  8.1 19.3 %collective-permute-start = (f32[2,256,512]{2,1,0:T(8,128)}, f32[2,256,512]{2,1,0:T(8,128)}, u32[]{:S(2)}, u32[]{:S(2)}) collective-permute-start(f32[2,256,512]{2,1,0:T(8,128)} %param.16), channel_id=1, source_target_pairs={{0,1},{1,0},{2,3},{3,2},{4,5},{5,4},{6,7},{7,6},{8,9},{9,8},{10,11... | collective-permute-start | bytes 3145736 | tf_op jit(solution)/shard_map/ppermute | solution.py:422
  89.7 36.1 %collective-permute-start.5 = (f32[2,4,128,128]{3,2,1,0:T(8,128)S(1)}, f32[2,4,128,128]{3,2,1,0:T(8,128)S(1)}, u32[]{:S(2)}, u32[]{:S(2)}) collective-permute-start(f32[2,4,128,128]{3,2,1,0:T(8,128)S(1)} %get-tuple-element.39), channel_id=1, source_target_pairs={{0,4},{2,6},{1,5},{3,7},{8,12},{10,14},{9,13},{11,15},{16,20},{18,... | collective-permute-start | bytes 1572872 | tf_op jit(solution)/shard_map/ppermute | solution.py:418
  92.5 33.3 %collective-permute-start.6 = (f32[2,4,128,128]{3,2,1,0:T(8,128)}, f32[2,4,128,128]{3,2,1,0:T(8,128)S(1)}, u32[]{:S(2)}, u32[]{:S(2)}) collective-permute-start(f32[2,4,128,128]{3,2,1,0:T(8,128)} %get-tuple-element.40), channel_id=1, source_target_pairs={{0,2},{2,4},{4,6},{1,3},{3,5},{5,7},{8,10},{10,12},{12,14},{9,11},... | collective-permute-start | bytes 1572872 | tf_op jit(solution)/shard_map/ppermute | solution.py:418
  157.0 19.6 %collective-permute-start.10 = (f32[512,1024]{1,0:T(8,128)}, f32[512,1024]{1,0:T(8,128)}, u32[]{:S(2)}, u32[]{:S(2)}) collective-permute-start(f32[512,1024]{1,0:T(8,128)} %convolution_add_fusion), channel_id=1, source_target_pairs={{0,1},{1,0},{2,3},{3,2},{4,5},{5,4},{6,7},{7,6},{8,9},{9,8},{10,11... | collective-permute-start | bytes 6291464 | tf_op jit(solution)/shard_map/ppermute | solution.py:422
  157.1 54.0 %collective-permute-start.13 = (f32[2,4,128,128]{3,2,1,0:T(8,128)}, f32[2,4,128,128]{3,2,1,0:T(8,128)}, u32[]{:S(2)}, u32[]{:S(2)}) collective-permute-start(f32[2,4,128,128]{3,2,1,0:T(8,128)} %get-tuple-element.40), channel_id=1, source_target_pairs={{2,0},{4,2},{6,4},{3,1},{5,3},{7,5},{10,8},{12,10},{14,12},{11,9},... | collective-permute-start | bytes 1572872 | tf_op jit(solution)/shard_map/ppermute | solution.py:418
  168.0 143.0 %collective-permute-start.31 = (f32[4,2,64,1408]{3,2,1,0:T(8,128)}, f32[4,2,64,1408]{3,2,1,0:T(8,128)}, u32[]{:S(2)}, u32[]{:S(2)}) collective-permute-start(f32[4,2,64,1408]{3,2,1,0:T(8,128)} %dynamic-slice_bitcast_fusion), channel_id=1, source_target_pairs={{0,4},{2,6},{4,0},{6,2},{1,5},{3,7},{5,1},{7,3},{8,12},{10,14},{12... | collective-permute-start | bytes 8650760 | tf_op jit(solution)/shard_map/ppermute | solution.py:454
  190.5 24.0 %collective-permute-start.11 = (f32[2,4,128,128]{3,2,1,0:T(8,128)}, f32[2,4,128,128]{3,2,1,0:T(8,128)}, u32[]{:S(2)}, u32[]{:S(2)}) collective-permute-start(f32[2,4,128,128]{3,2,1,0:T(8,128)} %get-tuple-element.45), channel_id=1, source_target_pairs={{2,0},{4,2},{6,4},{3,1},{5,3},{7,5},{10,8},{12,10},{14,12},{11,9},... | collective-permute-start | bytes 1572872 | tf_op jit(solution)/shard_map/ppermute | solution.py:418
  191.8 54.3 %collective-permute-start.12 = (f32[2,4,128,128]{3,2,1,0:T(8,128)}, f32[2,4,128,128]{3,2,1,0:T(8,128)}, u32[]{:S(2)}, u32[]{:S(2)}) collective-permute-start(f32[2,4,128,128]{3,2,1,0:T(8,128)} %get-tuple-element.45), channel_id=1, source_target_pairs={{4,0},{6,2},{5,1},{7,3},{12,8},{14,10},{13,9},{15,11},{20,16},{22,... | collective-permute-start | bytes 1572872 | tf_op jit(solution)/shard_map/ppermute | solution.py:418
  207.0 154.7 %collective-permute-start.29 = (f32[4,2,64,1408]{3,2,1,0:T(8,128)}, f32[4,2,64,1408]{3,2,1,0:T(8,128)}, u32[]{:S(2)}, u32[]{:S(2)}) collective-permute-start(f32[4,2,64,1408]{3,2,1,0:T(8,128)} %dynamic-slice_bitcast_fusion.1), channel_id=1, source_target_pairs={{0,2},{2,0},{4,6},{6,4},{1,3},{3,1},{5,7},{7,5},{8,10},{10,8},{12,... | collective-permute-start | bytes 8650760 | tf_op jit(solution)/shard_map/ppermute | solution.py:453
  211.1 106.6 %collective-permute-start.27 = (f32[4,2,64,512]{3,2,1,0:T(8,128)}, f32[4,2,64,512]{3,2,1,0:T(8,128)}, u32[]{:S(2)}, u32[]{:S(2)}) collective-permute-start(f32[4,2,64,512]{3,2,1,0:T(8,128)} %dynamic-slice_bitcast_fusion.6), channel_id=1, source_target_pairs={{0,4},{2,6},{4,0},{6,2},{1,5},{3,7},{5,1},{7,3},{8,12},{10,14},{12... | collective-permute-start | bytes 3145736 | tf_op jit(solution)/shard_map/ppermute | solution.py:454
  214.5 106.5 %collective-permute-start.25 = (f32[4,2,64,512]{3,2,1,0:T(8,128)}, f32[4,2,64,512]{3,2,1,0:T(8,128)}, u32[]{:S(2)}, u32[]{:S(2)}) collective-permute-start(f32[4,2,64,512]{3,2,1,0:T(8,128)} %dynamic-slice_bitcast_fusion.7), channel_id=1, source_target_pairs={{0,2},{2,0},{4,6},{6,4},{1,3},{3,1},{5,7},{7,5},{8,10},{10,8},{12,... | collective-permute-start | bytes 3145736 | tf_op jit(solution)/shard_map/ppermute | solution.py:453
  268.7 29.7 %collective-permute-start.14 = (f32[3,2,8,512]{3,2,1,0:T(8,128)}, f32[3,2,8,512]{3,2,1,0:T(8,128)}, u32[]{:S(2)}, u32[]{:S(2)}) collective-permute-start(f32[3,2,8,512]{3,2,1,0:T(8,128)} %get-tuple-element.55), channel_id=1, source_target_pairs={{2,0},{4,2},{6,4},{3,1},{5,3},{7,5},{10,8},{12,10},{14,12},{11,9},... | collective-permute-start | bytes 294920 | tf_op jit(solution)/shard_map/ppermute | solution.py:418
  306.2 47.3 %collective-permute-start.15 = (f32[512,1024]{1,0:T(8,128)S(1)}, f32[512,1024]{1,0:T(8,128)S(1)}, u32[]{:S(2)}, u32[]{:S(2)}) collective-permute-start(f32[512,1024]{1,0:T(8,128)S(1)} %add_add_fusion), channel_id=1, source_target_pairs={{0,1},{1,0},{2,3},{3,2},{4,5},{5,4},{6,7},{7,6},{8,9},{9,8},{10,11... | collective-permute-start | bytes 6291464 | tf_op jit(solution)/shard_map/ppermute | solution.py:422
  311.5 53.3 %collective-permute-start.19 = (f32[4,2,64,512]{3,2,1,0:T(8,128)}, f32[4,2,64,512]{3,2,1,0:T(8,128)}, u32[]{:S(2)}, u32[]{:S(2)}) collective-permute-start(f32[4,2,64,512]{3,2,1,0:T(8,128)} %dynamic-slice_bitcast_fusion.8), channel_id=1, source_target_pairs={{0,4},{2,6},{4,0},{6,2},{1,5},{3,7},{5,1},{7,3},{8,12},{10,14},{12... | collective-permute-start | bytes 3145736 | tf_op jit(solution)/shard_map/ppermute | solution.py:454
  322.4 27.8 %collective-permute-start.26 = (f32[4,64,512]{2,1,0:T(8,128)S(1)}, f32[4,64,512]{2,1,0:T(8,128)S(1)}, u32[]{:S(2)}, u32[]{:S(2)}) collective-permute-start(f32[4,64,512]{2,1,0:T(8,128)S(1)} %dynamic-slice_bitcast_fusion.13), channel_id=1, source_target_pairs={{0,4},{2,6},{4,0},{6,2},{1,5},{3,7},{5,1},{7,3},{8,12},{10,14},{12... | collective-permute-start | bytes 1572872 | tf_op jit(solution)/shard_map/ppermute | solution.py:457
  333.7 34.0 %collective-permute-start.17 = (f32[4,2,64,512]{3,2,1,0:T(8,128)}, f32[4,2,64,512]{3,2,1,0:T(8,128)}, u32[]{:S(2)}, u32[]{:S(2)}) collective-permute-start(f32[4,2,64,512]{3,2,1,0:T(8,128)} %dynamic-slice_bitcast_fusion.9), channel_id=1, source_target_pairs={{0,2},{2,0},{4,6},{6,4},{1,3},{3,1},{5,7},{7,5},{8,10},{10,8},{12,... | collective-permute-start | bytes 3145736 | tf_op jit(solution)/shard_map/ppermute | solution.py:453
  350.2 51.5 %collective-permute-start.32 = (f32[4,64,1408]{2,1,0:T(8,128)}, f32[4,64,1408]{2,1,0:T(8,128)}, u32[]{:S(2)}, u32[]{:S(2)}) collective-permute-start(f32[4,64,1408]{2,1,0:T(8,128)} %dynamic-slice_bitcast_fusion.3), channel_id=1, source_target_pairs={{0,2},{2,0},{4,6},{6,4},{1,3},{3,1},{5,7},{7,5},{8,10},{10,8},{12,... | collective-permute-start | bytes 4325384 | tf_op jit(solution)/shard_map/ppermute | solution.py:458
  359.2 159.2 %reduce-scatter.10.cloned.1.call-start = ((), (), s32[]{:S(2)}) async-start(), calls=%async_computation.7 | async-start | bytes 1310720 | tf_op jit(solution)/shard_map/reduce_scatter | solution.py:463
  361.6 158.6 %reduce-scatter.6.cloned.1.call-start = ((), (), s32[]{:S(2)}) async-start(), calls=%async_computation.5 | async-start | bytes 1310720 | tf_op jit(solution)/shard_map/reduce_scatter | solution.py:463
  367.6 32.8 %collective-permute-start.20 = (f32[4,64,512]{2,1,0:T(8,128)S(1)}, f32[4,64,512]{2,1,0:T(8,128)S(1)}, u32[]{:S(2)}, u32[]{:S(2)}) collective-permute-start(f32[4,64,512]{2,1,0:T(8,128)S(1)} %dynamic-slice_bitcast_fusion.16), channel_id=1, source_target_pairs={{0,2},{2,0},{4,6},{6,4},{1,3},{3,1},{5,7},{7,5},{8,10},{10,8},{12,... | collective-permute-start | bytes 1572872 | tf_op jit(solution)/shard_map/ppermute | solution.py:458
  369.4 31.1 %collective-permute-start.18 = (f32[4,64,512]{2,1,0:T(8,128)S(1)}, f32[4,64,512]{2,1,0:T(8,128)S(1)}, u32[]{:S(2)}, u32[]{:S(2)}) collective-permute-start(f32[4,64,512]{2,1,0:T(8,128)S(1)} %dynamic-slice_bitcast_fusion.17), channel_id=1, source_target_pairs={{0,4},{2,6},{4,0},{6,2},{1,5},{3,7},{5,1},{7,3},{8,12},{10,14},{12... | collective-permute-start | bytes 1572872 | tf_op jit(solution)/shard_map/ppermute | solution.py:457
  371.9 41.6 %collective-permute-start.30 = (f32[4,64,1408]{2,1,0:T(8,128)}, f32[4,64,1408]{2,1,0:T(8,128)}, u32[]{:S(2)}, u32[]{:S(2)}) collective-permute-start(f32[4,64,1408]{2,1,0:T(8,128)} %dynamic-slice_bitcast_fusion.4), channel_id=1, source_target_pairs={{0,4},{2,6},{4,0},{6,2},{1,5},{3,7},{5,1},{7,3},{8,12},{10,14},{12... | collective-permute-start | bytes 4325384 | tf_op jit(solution)/shard_map/ppermute | solution.py:457
  401.7 120.2 %reduce-scatter.12.cloned.1.call-start = ((), (), s32[]{:S(2)}) async-start(), calls=%async_computation.8 | async-start | bytes 3604480 | tf_op jit(solution)/shard_map/reduce_scatter | solution.py:463
  416.9 107.0 %reduce-scatter.8.cloned.1.call-start = ((), (), s32[]{:S(2)}) async-start(), calls=%async_computation.6 | async-start | bytes 655360 | tf_op jit(solution)/shard_map/reduce_scatter | solution.py:463
  427.4 29.1 %collective-permute-start.33 = (f32[4,2,64,640]{3,2,1,0:T(8,128)}, f32[4,2,64,640]{3,2,1,0:T(8,128)}, u32[]{:S(2)}, u32[]{:S(2)}) collective-permute-start(f32[4,2,64,640]{3,2,1,0:T(8,128)} %dynamic-slice_bitcast_fusion.5), channel_id=1, source_target_pairs={{0,2},{2,0},{4,6},{6,4},{1,3},{3,1},{5,7},{7,5},{8,10},{10,8},{12,... | collective-permute-start | bytes 3932168 | tf_op jit(solution)/shard_map/ppermute | solution.py:453
  432.9 37.7 %collective-permute-start.35 = (f32[4,2,64,768]{3,2,1,0:T(8,128)}, f32[4,2,64,768]{3,2,1,0:T(8,128)}, u32[]{:S(2)}, u32[]{:S(2)}) collective-permute-start(f32[4,2,64,768]{3,2,1,0:T(8,128)} %dynamic-slice_bitcast_fusion.2), channel_id=1, source_target_pairs={{0,4},{2,6},{4,0},{6,2},{1,5},{3,7},{5,1},{7,3},{8,12},{10,14},{12... | collective-permute-start | bytes 4718600 | tf_op jit(solution)/shard_map/ppermute | solution.py:454
  459.3 22.4 %collective-permute-start.23 = (f32[4,2,64,256]{3,2,1,0:T(8,128)S(1)}, f32[4,2,64,256]{3,2,1,0:T(8,128)S(1)}, u32[]{:S(2)}, u32[]{:S(2)}) collective-permute-start(f32[4,2,64,256]{3,2,1,0:T(8,128)S(1)} %dynamic-slice_bitcast_fusion.14), channel_id=1, source_target_pairs={{0,4},{2,6},{4,0},{6,2},{1,5},{3,7},{5,1},{7,3},{8,12},{10,14},{12... | collective-permute-start | bytes 1572872 | tf_op jit(solution)/shard_map/ppermute | solution.py:454
  460.6 43.4 %collective-permute-start.34 = (f32[4,64,640]{2,1,0:T(8,128)}, f32[4,64,640]{2,1,0:T(8,128)S(1)}, u32[]{:S(2)}, u32[]{:S(2)}) collective-permute-start(f32[4,64,640]{2,1,0:T(8,128)} %dynamic-slice_bitcast_fusion.11), channel_id=1, source_target_pairs={{0,4},{2,6},{4,0},{6,2},{1,5},{3,7},{5,1},{7,3},{8,12},{10,14},{12... | collective-permute-start | bytes 1966088 | tf_op jit(solution)/shard_map/ppermute | solution.py:457
  462.4 20.6 %collective-permute-start.21 = (f32[4,2,64,256]{3,2,1,0:T(8,128)S(1)}, f32[4,2,64,256]{3,2,1,0:T(8,128)S(1)}, u32[]{:S(2)}, u32[]{:S(2)}) collective-permute-start(f32[4,2,64,256]{3,2,1,0:T(8,128)S(1)} %dynamic-slice_bitcast_fusion.15), channel_id=1, source_target_pairs={{0,2},{2,0},{4,6},{6,4},{1,3},{3,1},{5,7},{7,5},{8,10},{10,8},{12,... | collective-permute-start | bytes 1572872 | tf_op jit(solution)/shard_map/ppermute | solution.py:453
  484.6 19.5 %collective-permute-start.36 = (f32[4,64,768]{2,1,0:T(8,128)}, f32[4,64,768]{2,1,0:T(8,128)}, u32[]{:S(2)}, u32[]{:S(2)}) collective-permute-start(f32[4,64,768]{2,1,0:T(8,128)} %dynamic-slice_bitcast_fusion.10), channel_id=1, source_target_pairs={{0,2},{2,0},{4,6},{6,4},{1,3},{3,1},{5,7},{7,5},{8,10},{10,8},{12,... | collective-permute-start | bytes 2359304 | tf_op jit(solution)/shard_map/ppermute | solution.py:458
  499.0 56.7 %reduce-scatter.14.cloned.1.call-start = ((), (), s32[]{:S(2)}) async-start(), calls=%async_computation.9 | async-start | bytes 1802240 | tf_op jit(solution)/shard_map/reduce_scatter | solution.py:463
  (108 other events, 1398.1 us)
Sparse Core Ops, SparseCore 0:
  359.4 147.9 all-reduce.6
Sparse Core Ops, SparseCore 1:
  362.1 27.1 reduce-scatter.9
  401.7 28.3 reduce-scatter.5
  432.4 54.7 reduce-scatter.11
  499.1 21.8 reduce-scatter.7
  524.0 31.6 reduce-scatter.13
